TPU v7x, 256 devices: a whole 4x4x8 slice. The times are simulated.
256 devices in a mesh: depth: 4 (over z_lo), freq: 64 (over z_hi, x, y, core).
Axes of the slice: x: 4, y: 4, z: 8 (z_hi: 2, z_lo: 4; z = z_hi * 4 + z_lo), core: 2. Of those that a mesh axis runs over, the one named last changes fastest.
Arguments:
- source: float32 [64, 2, 256, 256], P('freq'), may hold values from -6 to 6
- receiver: float32 [64, 2, 256, 256], P('freq'), may hold values from -16 to 16
- classes: int32 [4, 256, 256], P('depth'), may hold values from 0 to 15
- coef_table: float32 [16, 64, 2, 6], replicated, may hold values from -2 to 2, as said below
- freq_list: int32 [64], P('freq'), may hold values from 0 to 63, each once
Outputs:
- image: float32 [256, 4, 8, 256], P('freq', 'depth')
Inputs may be any that keep to these rules, and one draw needn't show every extreme that they name: `coef_table`: every entry lies within the stated bounds.
All inputs are finite; a program needn't handle non-finite values.
Results may differ from a plain program's by a relative error of at most 0.00011.
Values sent between devices are 32-bit elements; how exact they have to be, the bound alone decides.
No kernel may reach another device: no remote copies, remote signals or barrier semaphores. Data moves between devices by JAX's collectives and lax.ppermute only.
A program may use at most 64 MiB of HBM per device.

v0:
```python
import jax
import jax.numpy as jnp
from jax import lax
from jax.sharding import PartitionSpec as P

H = 8


def shifted(block, axis, distance):
    devices = range(lax.axis_size(axis))
    route = [(i - distance, i) for i in devices if i - distance in devices]
    return lax.ppermute(block, axis, route)


def mcclellan(field):
    widths = [(0, 0)] * (field.ndim - 2) + [(1, 1), (1, 1)]
    padded = jnp.pad(field, widths)
    axial_sum = (
        padded[..., 2:, 1:-1]
        + padded[..., :-2, 1:-1]
        + padded[..., 1:-1, 2:]
        + padded[..., 1:-1, :-2]
    )
    corner_sum = (
        padded[..., 2:, 2:] + padded[..., 2:, :-2] + padded[..., :-2, 2:] + padded[..., :-2, :-2]
    )
    return -0.5 * field + 0.25 * axial_sum + 0.125 * corner_sum


def apply_masked(field):
    moved = mcclellan(field)
    return moved


def extrapolate(fields, coeffs, keep=None):
    terms = coeffs.shape[3]
    earlier = fields
    current = apply_masked(fields)
    total_real = coeffs[:, :, 0, 0] * earlier[:, :, 0] - coeffs[:, :, 1, 0] * earlier[:, :, 1]
    total_imag = coeffs[:, :, 0, 0] * earlier[:, :, 1] + coeffs[:, :, 1, 0] * earlier[:, :, 0]
    for term_no in range(1, terms):
        total_real = (
            total_real
            + coeffs[:, :, 0, term_no] * current[:, :, 0]
            - coeffs[:, :, 1, term_no] * current[:, :, 1]
        )
        total_imag = (
            total_imag
            + coeffs[:, :, 0, term_no] * current[:, :, 1]
            + coeffs[:, :, 1, term_no] * current[:, :, 0]
        )
        if term_no + 1 < terms:
            following = 2.0 * apply_masked(current) - earlier
            earlier, current = (current, following)
    return jnp.stack([total_real, total_imag], axis=2)


def correlate(padded_levels, row_count, offset_total, scaling):
    margin = offset_total // 2
    offsets = []
    for offset_no in range(offset_total):
        shift_x = offset_no - margin
        src_part = padded_levels[:, 0, :, :, margin - shift_x : margin - shift_x + row_count]
        rec_part = padded_levels[:, 1, :, :, margin + shift_x : margin + shift_x + row_count]
        offsets.append(jnp.sum(src_part * rec_part, axis=(1, 2)))
    stacked = jnp.stack(offsets, axis=1)
    return jnp.transpose(stacked, (2, 0, 1, 3)) * scaling


def per_device(source, receiver, classes, coef_table, freq_list):
    section = lax.axis_index("depth")
    depth_count = lax.axis_size("depth")
    freq_count = lax.axis_size("freq")
    class_count = coef_table.shape[0]
    term_count = coef_table.shape[3]
    slot_count = source.shape[0]
    rows_x = source.shape[2]
    cols_y = source.shape[3]
    levels_here = classes.shape[0]
    offset_total = H
    margin = offset_total // 2
    scaling = float(slot_count * freq_count) ** (-0.5)
    chooser = (
        freq_list[:, None] == jnp.arange(coef_table.shape[1], dtype=jnp.int32)[None, :]
    ).astype(jnp.float32)
    local_table = jnp.einsum("fg,cgrk->frkc", chooser, coef_table, precision=lax.Precision.HIGHEST)
    imag_sign = jnp.array([1.0, -1.0], dtype=local_table.dtype)
    both_tables = jnp.stack([local_table * imag_sign[None, :, None, None], local_table])
    class_ids = jnp.arange(class_count, dtype=jnp.int32)[:, None]
    start_fields = jnp.stack([source, receiver])
    one_hots = [(classes[0].reshape(1, -1) == class_ids).astype(jnp.float32)]

    def run_slab(entering, slot_safe):
        slot_rows = both_tables.reshape(-1, class_count)
        fields = entering
        coeffs = jnp.dot(
            slot_rows,
            one_hots[0],
            precision=lax.Precision.HIGHEST,
            preferred_element_type=jnp.float32,
        )
        coeffs = coeffs.reshape(2, 1, 2, term_count, rows_x, cols_y)
        fields = extrapolate(fields, coeffs)
        levels = [fields]
        return (fields, jnp.stack(levels))

    def skip_slab(entering, slot_safe):
        return (
            jnp.zeros_like(entering),
            jnp.zeros((levels_here,) + entering.shape, entering.dtype),
        )

    stored = jnp.zeros((levels_here,) + start_fields.shape, start_fields.dtype)
    incoming = jnp.zeros((2, 1, 2, rows_x, cols_y), start_fields.dtype)
    round_total = slot_count + depth_count - 1
    for step_round in range(round_total):
        slot_now = step_round - section
        active = (slot_now >= 0) & (slot_now < slot_count)
        slot_safe = jnp.clip(slot_now, 0, slot_count - 1)
        entering = jnp.where(section == 0, start_fields, incoming)
        deepest, got_levels = lax.cond(active, run_slab, skip_slab, entering, slot_safe)
        updated = lax.dynamic_update_slice_in_dim(stored, got_levels, slot_safe, 2)
        stored = jnp.where(active, updated, stored)
        if step_round + 1 < round_total:
            incoming = shifted(deepest, "depth", 1)
    padded_levels = jnp.pad(stored, [(0, 0), (0, 0), (0, 0), (0, 0), (margin, margin), (0, 0)])
    terms = correlate(padded_levels, rows_x, offset_total, scaling)
    return lax.psum_scatter(terms, "freq", scatter_dimension=0, tiled=True)


def solution(mesh):
    placed = (
        P("freq", None, None, None),
        P("freq", None, None, None),
        P("depth", None, None),
        P(),
        P("freq"),
    )
    return jax.shard_map(
        per_device,
        mesh=mesh,
        in_specs=placed,
        out_specs=P("freq", "depth", None, None),
        check_vma=False,
    )
```

profile of v0, /device:TPU:32, one launch (start us, length us, event | category | flops | bytes accessed | tf_op | source)
XLA Modules:
  0.0 999.1 jit_solution(3084575799669628202)
XLA Ops:
  6.5 0.0 copy-start
  6.5 0.0 copy-start.2
  6.5 0.0 copy-start.3
  6.5 0.0 reduce-scatter.2.cloned.1.call-start
  7.3 0.1 copy-done
  7.4 0.4 fusion.26
  7.9 0.8 fusion.29
  8.6 1.1 copy.123
  9.7 2.2 fusion.24
  11.9 0.0 copy-done.2
  11.9 0.4 reshape_dynamic-update-slice_fusion.1
  12.3 0.0 copy-done.3
  12.3 0.4 reshape_dynamic-update-slice_fusion
  12.7 10.8 %conditional.4 = (f32[2,1,2,256,256]{4,1,3,2,0:T(1,128)}, f32[1,2,1,2,256,256]{5,2,4,3,1,0:T(1,128)S(1)}) conditional(s32[]{:T(128)} %convert_element_type.43, () %tuple.38, (f32[2,1,2,6,16]{4,3,2,0,1:T(8,128)S(1)}, f32[16,65536]{1,0:T(8,128)}, pred[]{:T(512)}, f32[2,1,2,256,256]{4,1,3,2,0:T(1,128)S(1)}) %tuple.39), branch_computations={%region_0.1_spmd, %region_1.2_spmd} | conditional | flops 328466432 | bytes 66061840 | solution.py:121
  12.7 1.5 broadcast.63
  14.2 0.5 broadcast.64
  23.6 4.1 collective-permute-start
  27.7 124.1 %collective-permute-done = f32[2,1,2,256,256]{4,1,3,2,0:T(1,128)S(1)} collective-permute-done((f32[2,1,2,256,256]{4,1,3,2,0:T(1,128)}, f32[2,1,2,256,256]{4,1,3,2,0:T(1,128)S(1)}, u32[]{:S(2)}, u32[]{:S(2)}) %collective-permute-start) | collective-permute-done | bytes 1048608 | tf_op jit(solution)/shard_map/ppermute | solution.py:12
  151.7 114.4 %conditional.5 = (f32[2,1,2,256,256]{4,1,3,2,0:T(1,128)}, f32[1,2,1,2,256,256]{5,2,4,3,1,0:T(1,128)S(1)}) conditional(s32[]{:T(128)} %convert_element_type.42, () %tuple.37, (f32[2,1,2,6,16]{4,3,2,0,1:T(8,128)S(1)}, f32[16,65536]{1,0:T(8,128)}, pred[]{:T(512)}, f32[2,1,2,256,256]{4,1,3,2,0:T(1,128)S(1)}, f32[2,1,2,256,256]{4,1,3,2,0:T(1,128)S(1)}) %tuple.40), branch_computations={%region_2.3_spmd, %region_3.4_spmd} | conditional | flops 328204288 | bytes 67110416 | solution.py:121
  151.7 3.4 copy.120
  155.2 9.5 fusion.8
  164.7 0.1 broadcast_select_fusion.1
  164.8 14.5 %multiply_add_fusion.2 = f32[2,1,2,256,256]{4,1,3,2,0:T(1,128)S(1)} fusion(f32[2,1,2,256,256]{4,1,3,2,0:T(1,128)S(1)} %bitcast.487), kind=kLoop, calls=%fused_computation.43 | loop fusion | flops 2883584 | bytes 2097152 | tf_op jit(solution)/shard_map/cond/branch_1_fun/add | solution.py:27
  179.4 14.2 %multiply_subtract_fusion.8 = f32[2,1,2,256,256]{4,1,3,2,0:T(1,128)S(1)} fusion(f32[2,1,2,256,256]{4,1,3,2,0:T(1,128)S(1)} %bitcast.488, f32[2,1,2,256,256]{4,1,3,2,0:T(1,128)S(1)} %multiply_add_fusion.2), kind=kLoop, calls=%fused_computation.41 | loop fusion | flops 3407872 | bytes 3145728 | tf_op jit(solution)/shard_map/cond/branch_1_fun/sub | solution.py:53
  193.6 28.6 %multiply_subtract_fusion.7 = f32[2,1,2,256,256]{4,1,3,2,0:T(1,128)S(1)} fusion(f32[2,1,2,256,256]{4,1,3,2,0:T(1,128)S(1)} %multiply_subtract_fusion.8, f32[2,1,2,256,256]{4,1,3,2,0:T(1,128)S(1)} %bitcast.489), kind=kLoop, calls=%fused_computation.39 | loop fusion | flops 6291456 | bytes 3145728 | tf_op jit(solution)/shard_map/cond/branch_1_fun/sub | solution.py:53
  222.2 14.2 %multiply_subtract_fusion.6 = f32[2,1,2,256,256]{4,1,3,2,0:T(1,128)S(1)} fusion(f32[2,1,2,256,256]{4,1,3,2,0:T(1,128)S(1)} %multiply_subtract_fusion.8, f32[2,1,2,256,256]{4,1,3,2,0:T(1,128)S(1)} %multiply_subtract_fusion.7), kind=kLoop, calls=%fused_computation.37 | loop fusion | flops 3407872 | bytes 3145728 | tf_op jit(solution)/shard_map/cond/branch_1_fun/sub | solution.py:53
  236.5 14.2 %multiply_subtract_fusion.5 = f32[2,1,2,256,256]{4,1,3,2,0:T(1,128)S(1)} fusion(f32[2,1,2,256,256]{4,1,3,2,0:T(1,128)S(1)} %multiply_subtract_fusion.7, f32[2,1,2,256,256]{4,1,3,2,0:T(1,128)S(1)} %multiply_subtract_fusion.6), kind=kLoop, calls=%fused_computation.35 | loop fusion | flops 3407872 | bytes 3145728 | tf_op jit(solution)/shard_map/cond/branch_1_fun/sub | solution.py:53
  250.7 6.0 multiply_add_fusion.3
  256.8 6.2 multiply_subtract_fusion.9
  263.0 2.0 pad_maximum_fusion.1
  264.9 0.9 fusion.35
  266.1 1.9 collective-permute-start.1
  268.1 22.2 %collective-permute-done.1 = f32[2,1,2,256,256]{4,1,3,2,0:T(1,128)} collective-permute-done((f32[2,1,2,256,256]{4,1,3,2,0:T(1,128)}, f32[2,1,2,256,256]{4,1,3,2,0:T(1,128)}, u32[]{:S(2)}, u32[]{:S(2)}) %collective-permute-start.1) | collective-permute-done | bytes 1048608 | tf_op jit(solution)/shard_map/ppermute | solution.py:12
  290.3 11.7 %conditional.6 = (f32[2,1,2,256,256]{4,1,3,2,0:T(1,128)}, f32[1,2,1,2,256,256]{5,2,4,3,1,0:T(1,128)}) conditional(s32[]{:T(128)} %convert_element_type.41, () %tuple.36, (f32[2,1,2,6,16]{4,3,2,0,1:T(8,128)S(1)}, f32[16,65536]{1,0:T(8,128)}, pred[]{:T(512)}, f32[2,1,2,256,256]{4,1,3,2,0:T(1,128)S(1)}, f32[2,1,2,256,256]{4,1,3,2,0:T(1,128)}) %tuple.41), branch_computations={%region_4.5_spmd, %region_5.6_spmd} | conditional | flops 328204288 | bytes 67110416 | solution.py:121
  290.3 1.6 broadcast.96
  291.8 1.5 broadcast.97
  301.9 107.0 %collective-permute-start.2 = (f32[2,1,2,256,256]{4,1,3,2,0:T(1,128)}, f32[2,1,2,256,256]{4,1,3,2,0:T(1,128)}, u32[]{:S(2)}, u32[]{:S(2)}) collective-permute-start(f32[2,1,2,256,256]{4,1,3,2,0:T(1,128)} %get-tuple-element.83), channel_id=1, source_target_pairs={{0,64},{64,128},{128,192},{1,65},{65,129},{129,193},{2,66},{66,130... | collective-permute-start | bytes 3145736 | tf_op jit(solution)/shard_map/ppermute | solution.py:12
  409.0 19.2 %collective-permute-done.2 = f32[2,1,2,256,256]{4,1,3,2,0:T(1,128)} collective-permute-done((f32[2,1,2,256,256]{4,1,3,2,0:T(1,128)}, f32[2,1,2,256,256]{4,1,3,2,0:T(1,128)}, u32[]{:S(2)}, u32[]{:S(2)}) %collective-permute-start.2) | collective-permute-done | bytes 1048608 | tf_op jit(solution)/shard_map/ppermute | solution.py:12
  428.1 4.7 conditional.7
  428.1 0.5 broadcast.112
  432.9 2.1 broadcast_select_fusion.7
  435.0 12.0 %multiply_reduce_fusion = (f32[256,256]{1,0:T(8,128)S(1)}, f32[256,256]{1,0:T(8,128)S(1)}, f32[256,256]{1,0:T(8,128)S(1)}, f32[256,256]{1,0:T(8,128)S(1)}, f32[2...) fusion(f32[1,2,1,2,256,256]{5,2,4,3,1,0:T(1,128)S(1)} %broadcast_select_fusion.7), kind=kLoop, calls=%fused_computation.128 | loop fusion | flops 1572864 | bytes 4194304 | tf_op jit(solution)/shard_map/reduce_sum | solution.py:65
  447.0 0.2 stack.83
  447.2 0.2 stack.84
  447.4 0.2 stack.85
  447.6 0.2 stack.86
  447.8 0.2 stack.87
  448.0 0.9 stack.88
  448.8 0.9 stack.89
  449.7 0.9 stack.90
  450.6 0.0 copy-start.1
  450.6 5.1 stack.91
  455.7 1.5 multiply_bitcast_fusion
  457.2 0.0 reduce-scatter.2.cloned.1.call-update
  457.2 534.8 %reduce-scatter.2.cloned.1.call-done = f32[4,1,8,256]{3,2,1,0:T(8,128)} async-done(((f32[256,1,8,256]{3,2,1,0:T(8,128)}), f32[4,1,8,256]{3,2,1,0:T(8,128)}) %reduce-scatter.2.cloned.1.call-update) | async-done | bytes 32784 | tf_op jit(solution)/shard_map/reduce_scatter | solution.py:128
  992.0 0.0 copy-done.1
  (2 shorter events, 0.0 us)
Async XLA Ops:
  6.5 0.9 copy-start
  6.5 5.4 copy-start.2
  6.5 5.8 copy-start.3
  6.5 985.5 %reduce-scatter.2.cloned.1.call-start = ((), (), s32[]{:S(2)}) async-start(), calls=%async_computation.1 | async-start | bytes 2129920 | tf_op jit(solution)/shard_map/reduce_scatter | solution.py:128
  23.6 128.2 %collective-permute-start = (f32[2,1,2,256,256]{4,1,3,2,0:T(1,128)}, f32[2,1,2,256,256]{4,1,3,2,0:T(1,128)S(1)}, u32[]{:S(2)}, u32[]{:S(2)}) collective-permute-start(f32[2,1,2,256,256]{4,1,3,2,0:T(1,128)} %get-tuple-element.81), channel_id=1, source_target_pairs={{0,64},{64,128},{128,192},{1,65},{65,129},{129,193},{2,66},{66,130... | collective-permute-start | bytes 3145736 | tf_op jit(solution)/shard_map/ppermute | solution.py:12
  266.1 24.1 %collective-permute-start.1 = (f32[2,1,2,256,256]{4,1,3,2,0:T(1,128)}, f32[2,1,2,256,256]{4,1,3,2,0:T(1,128)}, u32[]{:S(2)}, u32[]{:S(2)}) collective-permute-start(f32[2,1,2,256,256]{4,1,3,2,0:T(1,128)} %get-tuple-element.82), channel_id=1, source_target_pairs={{0,64},{64,128},{128,192},{1,65},{65,129},{129,193},{2,66},{66,130... | collective-permute-start | bytes 3145736 | tf_op jit(solution)/shard_map/ppermute | solution.py:12
  301.9 126.2 %collective-permute-start.2 = (f32[2,1,2,256,256]{4,1,3,2,0:T(1,128)}, f32[2,1,2,256,256]{4,1,3,2,0:T(1,128)}, u32[]{:S(2)}, u32[]{:S(2)}) collective-permute-start(f32[2,1,2,256,256]{4,1,3,2,0:T(1,128)} %get-tuple-element.83), channel_id=1, source_target_pairs={{0,64},{64,128},{128,192},{1,65},{65,129},{129,193},{2,66},{66,130... | collective-permute-start | bytes 3145736 | tf_op jit(solution)/shard_map/ppermute | solution.py:12
  450.6 541.4 %copy-start.1 = (f32[16,64,2,6]{1,2,3,0:T(2,128)S(1)}, f32[16,64,2,6]{1,2,3,0:T(2,128)}, u32[]{:S(2)}) copy-start(f32[16,64,2,6]{1,2,3,0:T(2,128)} %param.17) | copy-start | bytes 147460
Sparse Core Ops, SparseCore 0:
  457.4 534.5 reduce-scatter.1
where the time goes:
time: 1000 us; the launch traced here: 999 us
  waiting for transfers between devices  700 us (70%)
  other arithmetic  120 us (12%)
  starting transfers between devices  113 us (11%)
  loops' own time  21.8 us (2%)
  local copies, waits for them, and re-layouts  19.8 us (2%)
  between operations  14.6 us (1%)
    reduce_scatter x1, waiting for transfers between devices, per_device(): return lax.psum_scatter(terms, 'freq', scatter_dimension=0, tiled=True)  535 us
    ppermute x3, waiting for transfers between devices, shifted(): return lax.ppermute(block, axis, route)  165 us
    ppermute x3, starting transfers between devices, shifted(): return lax.ppermute(block, axis, route)  113 us
    sub x4, other arithmetic, extrapolate(): following = 2.0 * apply_masked(current) - earlier  71.3 us
    another operation x4, loops' own time, per_device(): lax.cond(active, run_slab, skip_slab, entering, slot_safe)  21.8 us
  transfers between devices with their start and end apart: 4, of which 4 were waited for; matrix products, arithmetic and copies ran while one was open for 0% of the time, Pallas kernels for 0%

commit v1 on v0

v1 whole, which is shorter than its diff:
```python
import functools
import jax
import jax.numpy as jnp
from jax import lax
from jax.experimental import pallas as pl
from jax.experimental.pallas import tpu as pltpu
from jax.sharding import PartitionSpec as P

AXES = ("depth", "freq")
H = 8
K = 6
Z = 4
NX = 256
NY = 256
CHUNK = 64
WIN = 112
HALO = 24
STEPS = WIN // 8
EXT = STEPS + 8
LANES = 128
HALVES = NY // LANES


def split(linear):
    d, f = divmod(linear, 64)
    return d, f >> 5, (f >> 3) & 3, (f >> 1) & 3, f & 1


def join(d, zh, x, y, c):
    return d * 64 + ((zh * 4 + x) * 4 + y) * 2 + c


def route(move):
    return [(i, join(*move(*split(i)))) for i in range(256)]


def along_z(step):
    def move(d, zh, x, y, c):
        z = (zh * 4 + d + step(c)) % 8
        return z & 3, z >> 2, x, y, c

    return route(move)


def first_axis(t):
    def move(d, zh, x, y, c):
        return (d, zh, (x + t) % 4, y, c) if c == 0 else (d, zh, x, (y + t) % 4, c)

    return route(move)


def second_axis(t):
    def move(d, zh, x, y, c):
        return (d, zh, x, (y + t) % 4, c) if c == 0 else (d, zh, (x + t) % 4, y, c)

    return route(move)


def to_owner(p):
    def move(q, zh, x, y, c):
        level = 2 * (p ^ zh) + ((x >> 1) ^ (q & 1))
        return level, q >> 1, 2 * (q & 1) + (x & 1), y, c

    return route(move)


CORE_SWAP = route(lambda d, zh, x, y, c: (d, zh, x, y, 1 - c))


def window_start(q):
    return jnp.clip(CHUNK * q - HALO, 0, NX - WIN)


def kernel(place, src, rec, c0, c1, c2, c3, table, out, raw, cls, field, terms, img, in_sem, cls_sem, out_sem):
    q, x_at, y_at, core = place[0], place[1], place[2], place[3]
    start = pl.multiple_of(place[4], 8)
    loads = []
    for n, ref in enumerate((src, rec)):
        for half in range(HALVES):
            lanes = pl.ds(half * LANES, LANES)
            cp = pltpu.make_async_copy(ref.at[0, :, pl.ds(start, WIN), lanes], raw.at[n, :, half], in_sem.at[n, half])
            cp.start()
            loads.append(cp)
    cls_loads = []
    for n, ref in enumerate((c0, c1, c2, c3)):
        for half in range(HALVES):
            lanes = pl.ds(half * LANES, LANES)
            cp = pltpu.make_async_copy(ref.at[:, lanes], cls.at[place[5 + n], half], cls_sem.at[n, half])
            cp.start()
            cls_loads.append(cp)
    for cp in loads:
        cp.wait()

    lane = lax.broadcasted_iota(jnp.int32, (8, LANES), 1)
    sub = lax.broadcasted_iota(jnp.int32, (8, LANES), 0)
    first_lane, last_lane = lane == 0, lane == LANES - 1
    zero = jnp.zeros((8, LANES), jnp.float32)

    def from_above(v):
        return jnp.where(sub == 0, 0.0, pltpu.roll(v, 1, 0))

    def from_below(v):
        return jnp.where(sub == 7, 0.0, pltpu.roll(v, 7, 0))

    def left(lo, hi):
        rl, rh = pltpu.roll(lo, 1, 1), pltpu.roll(hi, 1, 1)
        return jnp.where(first_lane, zero, rl), jnp.where(first_lane, rl, rh)

    def right(lo, hi):
        rl, rh = pltpu.roll(lo, LANES - 1, 1), pltpu.roll(hi, LANES - 1, 1)
        return jnp.where(last_lane, rh, rl), jnp.where(last_lane, zero, rh)

    for comp in range(4):
        for r in range(STEPS):
            for half in range(HALVES):
                v = raw[comp // 2, comp % 2, half, pl.ds(r, 8, stride=STEPS), :]
                field[comp, half, 4 + r] = -v if comp == 1 else v
    for cp in cls_loads:
        cp.wait()

    def piece_copy(level, slot, i):
        c_o, y_o, ix = i & 1, (i >> 1) & 3, i >> 3
        lb, e = level >> 1, level & 1
        x_o = 2 * (e ^ (q & 1)) + ix
        dx, dy = (x_o - x_at) & 3, (y_o - y_at) & 3
        t, u = (dx, dy) if c_o == 0 else (dy, dx)
        at = (((c_o ^ core) * 4 + t) * 4 + u) * 2 + lb
        rows = pl.multiple_of((CHUNK * q - start + 4 * i) * H, 32)
        return pltpu.make_async_copy(img.at[slot, :, pl.ds(rows, 4 * H), :], out.at[at], out_sem.at[slot])

    def level_body(level, carry):
        slot = level & 1

        for k in range(1, K):
            for comp in range(4):
                def cur(r, half):
                    return field[comp, half, 4 + r] if k == 1 else terms[k - 2, comp, half, r]

                prev = [None, None]
                here = [cur(0, half) for half in range(HALVES)]
                above = [from_above(cur(STEPS - 1, half)) for half in range(HALVES)]
                top = here
                for r in range(STEPS):
                    if r < STEPS - 1:
                        below = [cur(r + 1, half) for half in range(HALVES)]
                    else:
                        below = [from_below(v) for v in top]
                    g, rest = [], []
                    for half in range(HALVES):
                        h = 0.5 * (above[half] + below[half])
                        g.append(h + here[half])
                        rest.append(h - here[half])
                    gl, gr = left(*g), right(*g)
                    for half in range(HALVES):
                        w = 0.5 * (gl[half] + gr[half]) + rest[half]
                        if k == 1:
                            w = 0.5 * w
                        elif k == 2:
                            w = w - field[comp, half, 4 + r]
                        else:
                            w = w - terms[k - 3, comp, half, r]
                        terms[k - 1, comp, half, r] = w
                    above, here = here, below

        def combine(r, carry):
            for half in range(HALVES):
                ids = cls[level, half, pl.ds(r, 8, stride=STEPS), :]
                coef = [
                    jnp.take_along_axis(table[n], ids, axis=1, mode="promise_in_bounds") for n in range(2 * K)
                ]
                p, s = [], []
                for comp in range(4):
                    vals = [field[comp, half, 4 + r]] + [terms[k, comp, half, r] for k in range(K - 1)]
                    a, b = coef[0] * vals[0], coef[K] * vals[0]
                    for k in range(1, K):
                        a = a + coef[k] * vals[k]
                        b = b + coef[K + k] * vals[k]
                    p.append(a)
                    s.append(b)
                for pair in range(2):
                    field[2 * pair, half, 4 + r] = p[2 * pair] - s[2 * pair + 1]
                    field[2 * pair + 1, half, 4 + r] = p[2 * pair + 1] + s[2 * pair]
            return carry

        lax.fori_loop(0, STEPS, combine, 0)
        for comp in range(4):
            for half in range(HALVES):
                for r in range(4):
                    field[comp, half, r] = from_above(field[comp, half, STEPS + r])
                    field[comp, half, STEPS + 4 + r] = from_below(field[comp, half, 4 + r])

        @pl.when(level >= 2)
        def _():
            for i in range(16):
                piece_copy(level - 2, slot, i).wait()

        def image(r, carry):
            for half in range(HALVES):
                for j in range(H):
                    h = j - H // 2
                    a = 4 + r - h
                    b = 4 + r + h
                    val = field[0, half, a] * field[2, half, b] - field[1, half, a] * field[3, half, b]
                    img[slot, half, pl.ds(r * H + j, 8, stride=STEPS * H), :] = val
            return carry

        lax.fori_loop(0, STEPS, image, 0)
        for i in range(16):
            piece_copy(level, slot, i).start()
        return carry

    lax.fori_loop(0, Z, level_body, 0)
    for level in (Z - 2, Z - 1):
        for i in range(16):
            piece_copy(level, level & 1, i).wait()


def images(place, source, receiver, class_windows, table):
    anyspace = pl.BlockSpec(memory_space=pl.ANY)
    return pl.pallas_call(
        kernel,
        out_shape=jax.ShapeDtypeStruct((64, HALVES, 4 * H, LANES), jnp.float32),
        in_specs=[pl.BlockSpec(memory_space=pltpu.SMEM)] + [anyspace] * 6 + [pl.BlockSpec(memory_space=pltpu.VMEM)],
        out_specs=anyspace,
        scratch_shapes=[
            pltpu.VMEM((2, 2, HALVES, WIN, LANES), jnp.float32),
            pltpu.VMEM((Z, HALVES, WIN, LANES), jnp.int32),
            pltpu.VMEM((4, HALVES, EXT, 8, LANES), jnp.float32),
            pltpu.VMEM((K - 1, 4, HALVES, STEPS, 8, LANES), jnp.float32),
            pltpu.VMEM((2, HALVES, WIN * H, LANES), jnp.float32),
            pltpu.SemaphoreType.DMA((2, HALVES)),
            pltpu.SemaphoreType.DMA((4, HALVES)),
            pltpu.SemaphoreType.DMA((2,)),
        ],
    )(place, source, receiver, *class_windows, table)


def per_device(source, receiver, classes, coef_table, freq_list):
    q = lax.axis_index("depth")
    f = lax.axis_index("freq")
    zh, x_at, y_at, core = f >> 5, (f >> 3) & 3, (f >> 1) & 3, f & 1

    def window(target):
        return lax.dynamic_slice(classes[0], (window_start(target & 3), 0), (WIN, NY))

    opposite = window(q + 2)
    class_windows = [
        window(q),
        lax.ppermute(window(q + 1), AXES, along_z(lambda c: 1)),
        lax.ppermute(window(q - 1), AXES, along_z(lambda c: -1)),
        lax.ppermute(opposite, AXES, along_z(lambda c: 2 if c == 0 else -2)),
    ]
    levels = [q, (q - 1) & 3, (q + 1) & 3, (q + 2) & 3]
    mine = lax.dynamic_slice_in_dim(coef_table, freq_list[0], 1, axis=1)[:, 0]
    rows = jnp.transpose(mine, (1, 2, 0)).reshape(2 * K, 1, -1)
    table = jnp.broadcast_to(jnp.pad(rows, [(0, 0), (0, 0), (0, LANES - rows.shape[2])]), (2 * K, 8, LANES))
    place = jnp.stack([q, x_at, y_at, core, window_start(q)] + levels).astype(jnp.int32)
    terms = images(place, source, receiver, class_windows, table)

    mine = terms[:32] + lax.ppermute(terms[32:], AXES, CORE_SWAP)
    for axis in (first_axis, second_axis):
        part = mine.shape[0] // 4
        got = [lax.ppermute(mine[t * part : (t + 1) * part], AXES, axis(t)) for t in (1, 2, 3)]
        mine = mine[:part] + got[0] + got[1] + got[2]
    sent = [lax.dynamic_index_in_dim(mine, p ^ zh, 0, keepdims=False) for p in (0, 1)]
    total = lax.ppermute(sent[0], AXES, to_owner(0)) + lax.ppermute(sent[1], AXES, to_owner(1))
    scaling = 64.0 ** -0.5
    image = (total * scaling).reshape(HALVES, 4, H, LANES)
    return jnp.transpose(image, (1, 2, 0, 3)).reshape(4, 1, H, NY)


def solution(mesh):
    placed = (
        P("freq", None, None, None),
        P("freq", None, None, None),
        P("depth", None, None),
        P(),
        P("freq"),
    )
    return jax.shard_map(
        per_device,
        mesh=mesh,
        in_specs=placed,
        out_specs=P("freq", "depth", None, None),
        check_vma=False,
    )
```

time: 1000 us -> 71.5 us (0.07)
  waiting for transfers between devices: 700 us -> 16.9 us
  other arithmetic: 120 us -> 1 us
  starting transfers between devices: 113 us -> 29 us
  loops' own time: 21.8 us -> 0 us
  Pallas kernels: 0 us -> 17.6 us
  local copies, waits for them, and re-layouts: 19.8 us -> 4.94 us
  between operations: 14.6 us -> 0.8 us
    reduce_scatter x1 -> x0, waiting for transfers between devices: 535 us -> none  [per_device(): return lax.psum_scatter(terms, 'freq', scatter_dimension=0, tiled=True)]
    ppermute x3 -> x12, waiting for transfers between devices: 165 us -> 16.9 us  [the longest x6 8.59 us: per_device(): lax.ppermute(mine[t * part:(t + 1) * part], AXES, axis(t))]
    ppermute x3 -> x12, starting transfers between devices: 113 us -> 29 us  [the longest x6 11.7 us: per_device(): lax.ppermute(mine[t * part:(t + 1) * part], AXES, axis(t))]
    sub x5 -> x0, other arithmetic: 77.5 us -> none  [the longest x4 71.3 us: extrapolate(): following = 2.0 * apply_masked(current) - earlier]
    another operation x4 -> x0, loops' own time: 21.8 us -> none  [per_device(): lax.cond(active, run_slab, skip_slab, entering, slot_safe)]
    add x2 -> x3, other arithmetic: 20.6 us -> 0.38 us  [the longest x1 0.26 us: per_device(): mine = terms[:32] + lax.ppermute(terms[32:], AXES, CORE_SWAP)]
    pallas_call x0 -> x1, Pallas kernels: none -> 17.6 us  [images(): pl.pallas_call(kernel, out_shape=jax.ShapeDtypeStruct((64, HALVES, 4 * H,...]
    another operation x15 -> x1, local copies, waits for them, and re-layouts: 14.8 us -> 0.61 us  [per_device(): jnp.stack([q, x_at, y_at, core, window_start(q)] + levels).astype(jnp.int32)]
  transfers between devices with their start and end apart: 4 -> 12, of which waited for: 4 -> 7; matrix products, arithmetic and copies ran while one was open for 0% -> 1% of each run, Pallas kernels for 0% -> 0%
where the time goes in v1:
time: 71.5 us; the launch traced here: 70.2 us
  starting transfers between devices  29 us (41%)
  Pallas kernels  17.6 us (25%)
  waiting for transfers between devices  16.9 us (24%)
  local copies, waits for them, and re-layouts  4.94 us (7%)
  other arithmetic  1 us (1%)
  between operations  0.8 us (1%)
    pallas_call x1, Pallas kernels, images(): pl.pallas_call(kernel, out_shape=jax.ShapeDtypeStruct((64, HALVES, 4 * H,...  17.6 us
    ppermute x6, starting transfers between devices, per_device(): lax.ppermute(mine[t * part:(t + 1) * part], AXES, axis(t))  11.7 us
    ppermute x6, waiting for transfers between devices, per_device(): lax.ppermute(mine[t * part:(t + 1) * part], AXES, axis(t))  8.59 us
    ppermute x1, starting transfers between devices, per_device(): lax.ppermute(sent[1], AXES, to_owner(1))  5.82 us
    ppermute x1, starting transfers between devices, per_device(): lax.ppermute(sent[0], AXES, to_owner(0))  4.87 us
    ppermute x1, starting transfers between devices, per_device(): lax.ppermute(opposite, AXES, along_z(lambda c: 2 if c == 0 else -2))  4.38 us
    ppermute x1, waiting for transfers between devices, per_device(): lax.ppermute(sent[1], AXES, to_owner(1))  3.59 us
    ppermute x1, waiting for transfers between devices, per_device(): mine = terms[:32] + lax.ppermute(terms[32:], AXES, CORE_SWAP)  2.52 us
  transfers between devices with their start and end apart: 12, of which 7 were waited for; matrix products, arithmetic and copies ran while one was open for 1% of the time, Pallas kernels for 0%

profile of v1, /device:TPU:32, one launch (start us, length us, event | category | flops | bytes accessed | tf_op | source)
XLA Modules:
  0.0 70.2 jit_solution(10532015483246257274)
XLA Ops:
  0.0 0.0 copy-start
  0.0 1.8 %dynamic-slice_bitcast_fusion = (s32[112,256]{1,0:T(8,128)S(1)}, s32[112,256]{1,0:T(8,128)S(1)}, s32[112,256]{1,0:T(8,128)}, s32[112,256]{1,0:T(8,128)S(1)}) fusion(s32[1,256,256]{2,1,0:T(8,128)} %param.7, s32[]{:T(128)S(6)} %min.20, s32[]{:T(128)S(6)} %min.18, s32[]{:T(128)S(6)} %min.17, s32[]{:T(128)S(6)} %min.19), kind=kLoop, calls=%fused_computation.4 | loop fusion | bytes 917520 | tf_op jit(solution)/shard_map/dynamic_slice | solution.py:244
  1.8 1.9 %collective-permute-start = (s32[112,256]{1,0:T(8,128)S(1)}, s32[112,256]{1,0:T(8,128)S(1)}, u32[]{:S(2)}, u32[]{:S(2)}) collective-permute-start(s32[112,256]{1,0:T(8,128)S(1)} %get-tuple-element.12), channel_id=1, source_target_pairs={{0,64},{1,65},{2,66},{3,67},{4,68},{5,69},{6,70},{7,71},{8,72},{9,... | collective-permute-start | bytes 344072 | tf_op jit(solution)/shard_map/ppermute | solution.py:249
  3.7 0.1 collective-permute-start.1
  3.8 4.4 %collective-permute-start.2 = (s32[112,256]{1,0:T(8,128)S(1)}, s32[112,256]{1,0:T(8,128)S(1)}, u32[]{:S(2)}, u32[]{:S(2)}) collective-permute-start(s32[112,256]{1,0:T(8,128)S(1)} %get-tuple-element.11), channel_id=1, source_target_pairs={{0,128},{1,161},{2,130},{3,163},{4,132},{5,165},{6,134},{7,167},{8... | collective-permute-start | bytes 344072 | tf_op jit(solution)/shard_map/ppermute | solution.py:251
  8.8 0.0 copy-done
  8.9 0.2 constant_dynamic-slice_fusion
  9.0 0.1 copy.8
  9.2 0.6 stack.36.place
  9.8 0.0 collective-permute-done.c1
  9.8 0.0 copy-start.2
  9.8 0.0 collective-permute-done.1.c2
  9.8 0.0 copy-start.3
  9.8 2.1 %collective-permute-done.2.c3 = s32[112,256]{1,0:T(8,128)S(1)} collective-permute-done((s32[112,256]{1,0:T(8,128)S(1)}, s32[112,256]{1,0:T(8,128)S(1)}, u32[]{:S(2)}, u32[]{:S(2)}) %collective-permute-start.2) | collective-permute-done | bytes 114720 | tf_op jit(solution)/shard_map/ppermute | solution.py:251
  12.0 0.0 copy-start.4
  12.0 0.7 broadcast_in_dim.8.table
  12.7 0.0 copy-done.2
  12.7 0.0 copy-done.3
  12.7 0.0 copy-done.4
  12.7 17.6 %shard_map.55 = f32[64,2,32,128]{3,2,1,0:T(8,128)} custom-call(s32[9]{0:T(128)} %stack.36.place, f32[1,2,256,256]{3,2,1,0:T(8,128)} %src.1, f32[1,2,256,256]{3,2,1,0:T(8,128)} %rec.1, s32[112,256]{1,0:T(8,128)} %get-tuple-element.13.c0, s32[112,256]{1,0:T(8,128)} %copy-done.2, s32[112,256]{1,0:T(8,128)} %copy-done.3, s32[112,256]{1,0:T(8,128)} %copy-done.4, ...), custom_call_target="tpu_custom_call" | custom-call | tf_op jit(solution)/shard_map/pallas_call | solution.py:220
  30.3 0.0 copy-start.1
  30.3 1.4 %slice.41 = f32[32,2,32,128]{3,2,1,0:T(8,128)S(1)} slice(f32[64,2,32,128]{3,2,1,0:T(8,128)} %shard_map.55), slice={[32:64], [0:2], [0:32], [0:128]} | slice | bytes 2097152 | tf_op jit(solution)/shard_map/slice | solution.py:260
  31.7 0.2 collective-permute-start.3
  32.0 2.5 %collective-permute-done.3 = f32[32,2,32,128]{3,2,1,0:T(8,128)S(1)} collective-permute-done((f32[32,2,32,128]{3,2,1,0:T(8,128)S(1)}, f32[32,2,32,128]{3,2,1,0:T(8,128)S(1)}, u32[]{:S(2)}, u32[]{:S(2)}) %collective-permute-start.3) | collective-permute-done | bytes 1048608 | tf_op jit(solution)/shard_map/ppermute | solution.py:260
  34.5 0.0 copy-done.1
  34.5 0.3 slice_add_fusion
  34.8 0.1 fusion.4
  34.8 1.6 %collective-permute-start.4 = (f32[8,2,32,128]{3,2,1,0:T(8,128)S(1)}, f32[8,2,32,128]{3,2,1,0:T(8,128)S(1)}, u32[]{:S(2)}, u32[]{:S(2)}) collective-permute-start(f32[8,2,32,128]{3,2,1,0:T(8,128)S(1)} %get-tuple-element.5), channel_id=1, source_target_pairs={{0,8},{1,3},{2,10},{3,5},{4,12},{5,7},{6,14},{7,1},{8,16},{9,11},{... | collective-permute-start | bytes 786440 | tf_op jit(solution)/shard_map/ppermute | solution.py:263
  36.4 2.8 %collective-permute-start.5 = (f32[8,2,32,128]{3,2,1,0:T(8,128)S(1)}, f32[8,2,32,128]{3,2,1,0:T(8,128)S(1)}, u32[]{:S(2)}, u32[]{:S(2)}) collective-permute-start(f32[8,2,32,128]{3,2,1,0:T(8,128)S(1)} %get-tuple-element.7), channel_id=1, source_target_pairs={{0,16},{1,5},{2,18},{3,7},{4,20},{5,1},{6,22},{7,3},{8,24},{9,13},... | collective-permute-start | bytes 786440 | tf_op jit(solution)/shard_map/ppermute | solution.py:263
  39.2 1.5 %collective-permute-start.6 = (f32[8,2,32,128]{3,2,1,0:T(8,128)S(1)}, f32[8,2,32,128]{3,2,1,0:T(8,128)S(1)}, u32[]{:S(2)}, u32[]{:S(2)}) collective-permute-start(f32[8,2,32,128]{3,2,1,0:T(8,128)S(1)} %get-tuple-element.6), channel_id=1, source_target_pairs={{0,24},{1,7},{2,26},{3,1},{4,28},{5,3},{6,30},{7,5},{8,0},{9,15},{... | collective-permute-start | bytes 786440 | tf_op jit(solution)/shard_map/ppermute | solution.py:263
  40.6 1.9 %collective-permute-done.4 = f32[8,2,32,128]{3,2,1,0:T(8,128)S(1)} collective-permute-done((f32[8,2,32,128]{3,2,1,0:T(8,128)S(1)}, f32[8,2,32,128]{3,2,1,0:T(8,128)S(1)}, u32[]{:S(2)}, u32[]{:S(2)}) %collective-permute-start.4) | collective-permute-done | bytes 262176 | tf_op jit(solution)/shard_map/ppermute | solution.py:263
  42.5 3.8 %collective-permute-done.5 = f32[8,2,32,128]{3,2,1,0:T(8,128)S(1)} collective-permute-done((f32[8,2,32,128]{3,2,1,0:T(8,128)S(1)}, f32[8,2,32,128]{3,2,1,0:T(8,128)S(1)}, u32[]{:S(2)}, u32[]{:S(2)}) %collective-permute-start.5) | collective-permute-done | bytes 262176 | tf_op jit(solution)/shard_map/ppermute | solution.py:263
  46.3 0.0 collective-permute-done.6
  46.3 0.1 fusion.1
  46.4 1.7 %collective-permute-start.7 = (f32[2,2,32,128]{3,2,1,0:T(8,128)S(1)}, f32[2,2,32,128]{3,2,1,0:T(8,128)S(1)}, u32[]{:S(2)}, u32[]{:S(2)}) collective-permute-start(f32[2,2,32,128]{3,2,1,0:T(8,128)S(1)} %get-tuple-element.8), channel_id=1, source_target_pairs={{0,2},{1,9},{2,4},{3,11},{4,6},{5,13},{6,0},{7,15},{8,10},{9,17},{... | collective-permute-start | bytes 196616 | tf_op jit(solution)/shard_map/ppermute | solution.py:263
  48.1 2.9 %collective-permute-start.8 = (f32[2,2,32,128]{3,2,1,0:T(8,128)S(1)}, f32[2,2,32,128]{3,2,1,0:T(8,128)S(1)}, u32[]{:S(2)}, u32[]{:S(2)}) collective-permute-start(f32[2,2,32,128]{3,2,1,0:T(8,128)S(1)} %get-tuple-element.10), channel_id=1, source_target_pairs={{0,4},{1,17},{2,6},{3,19},{4,0},{5,21},{6,2},{7,23},{8,12},{9,25},... | collective-permute-start | bytes 196616 | tf_op jit(solution)/shard_map/ppermute | solution.py:263
  51.0 1.4 %collective-permute-start.9 = (f32[2,2,32,128]{3,2,1,0:T(8,128)S(1)}, f32[2,2,32,128]{3,2,1,0:T(8,128)S(1)}, u32[]{:S(2)}, u32[]{:S(2)}) collective-permute-start(f32[2,2,32,128]{3,2,1,0:T(8,128)S(1)} %get-tuple-element.9), channel_id=1, source_target_pairs={{0,6},{1,25},{2,0},{3,27},{4,2},{5,29},{6,4},{7,31},{8,14},{9,1},{... | collective-permute-start | bytes 196616 | tf_op jit(solution)/shard_map/ppermute | solution.py:263
  52.4 0.0 collective-permute-done.7
  52.4 1.6 %collective-permute-done.8 = f32[2,2,32,128]{3,2,1,0:T(8,128)S(1)} collective-permute-done((f32[2,2,32,128]{3,2,1,0:T(8,128)S(1)}, f32[2,2,32,128]{3,2,1,0:T(8,128)S(1)}, u32[]{:S(2)}, u32[]{:S(2)}) %collective-permute-start.8) | collective-permute-done | bytes 65568 | tf_op jit(solution)/shard_map/ppermute | solution.py:263
  53.9 1.3 %collective-permute-done.9 = f32[2,2,32,128]{3,2,1,0:T(8,128)S(1)} collective-permute-done((f32[2,2,32,128]{3,2,1,0:T(8,128)S(1)}, f32[2,2,32,128]{3,2,1,0:T(8,128)S(1)}, u32[]{:S(2)}, u32[]{:S(2)}) %collective-permute-start.9) | collective-permute-done | bytes 65568 | tf_op jit(solution)/shard_map/ppermute | solution.py:263
  55.3 4.9 %collective-permute-start.10 = (f32[2,32,128]{2,1,0:T(8,128)S(1)}, f32[2,32,128]{2,1,0:T(8,128)S(1)}, u32[]{:S(2)}, u32[]{:S(2)}) collective-permute-start(f32[2,32,128]{2,1,0:T(8,128)S(1)} %get-tuple-element.16), channel_id=1, source_target_pairs={{0,0},{1,1},{2,2},{3,3},{4,4},{5,5},{6,6},{7,7},{8,8},{9,9},{10,10... | collective-permute-start | bytes 98312 | tf_op jit(solution)/shard_map/ppermute | solution.py:266
  60.2 5.8 %collective-permute-start.11 = (f32[2,32,128]{2,1,0:T(8,128)S(1)}, f32[2,32,128]{2,1,0:T(8,128)S(1)}, u32[]{:S(2)}, u32[]{:S(2)}) collective-permute-start(f32[2,32,128]{2,1,0:T(8,128)S(1)} %get-tuple-element.15), channel_id=1, source_target_pairs={{0,128},{1,129},{2,130},{3,131},{4,132},{5,133},{6,134},{7,135},{8... | collective-permute-start | bytes 98312 | tf_op jit(solution)/shard_map/ppermute | solution.py:266
  66.0 0.0 collective-permute-done.10
  66.0 3.6 %collective-permute-done.11 = f32[2,32,128]{2,1,0:T(8,128)S(1)} collective-permute-done((f32[2,32,128]{2,1,0:T(8,128)S(1)}, f32[2,32,128]{2,1,0:T(8,128)S(1)}, u32[]{:S(2)}, u32[]{:S(2)}) %collective-permute-start.11) | collective-permute-done | bytes 32800 | tf_op jit(solution)/shard_map/ppermute | solution.py:266
  69.6 0.6 copy_bitcast_fusion
  (6 shorter events, 0.1 us)
Async XLA Ops:
  0.0 8.9 %copy-start = (f32[16,64,2,6]{1,2,3,0:T(2,128)S(1)}, f32[16,64,2,6]{1,2,3,0:T(2,128)}, u32[]{:S(2)}) copy-start(f32[16,64,2,6]{1,2,3,0:T(2,128)} %param.8) | copy-start | bytes 147460
  1.8 8.0 %collective-permute-start = (s32[112,256]{1,0:T(8,128)S(1)}, s32[112,256]{1,0:T(8,128)S(1)}, u32[]{:S(2)}, u32[]{:S(2)}) collective-permute-start(s32[112,256]{1,0:T(8,128)S(1)} %get-tuple-element.12), channel_id=1, source_target_pairs={{0,64},{1,65},{2,66},{3,67},{4,68},{5,69},{6,70},{7,71},{8,72},{9,... | collective-permute-start | bytes 344072 | tf_op jit(solution)/shard_map/ppermute | solution.py:249
  3.7 6.1 %collective-permute-start.1 = (s32[112,256]{1,0:T(8,128)S(1)}, s32[112,256]{1,0:T(8,128)S(1)}, u32[]{:S(2)}, u32[]{:S(2)}) collective-permute-start(s32[112,256]{1,0:T(8,128)S(1)} %get-tuple-element.14), channel_id=1, source_target_pairs={{0,224},{1,225},{2,226},{3,227},{4,228},{5,229},{6,230},{7,231},{8... | collective-permute-start | bytes 344072 | tf_op jit(solution)/shard_map/ppermute | solution.py:250
  3.8 8.2 %collective-permute-start.2 = (s32[112,256]{1,0:T(8,128)S(1)}, s32[112,256]{1,0:T(8,128)S(1)}, u32[]{:S(2)}, u32[]{:S(2)}) collective-permute-start(s32[112,256]{1,0:T(8,128)S(1)} %get-tuple-element.11), channel_id=1, source_target_pairs={{0,128},{1,161},{2,130},{3,163},{4,132},{5,165},{6,134},{7,167},{8... | collective-permute-start | bytes 344072 | tf_op jit(solution)/shard_map/ppermute | solution.py:251
  9.8 2.8 %copy-start.2 = (s32[112,256]{1,0:T(8,128)}, s32[112,256]{1,0:T(8,128)S(1)}, u32[]{:S(2)}) copy-start(s32[112,256]{1,0:T(8,128)S(1)} %collective-permute-done.c1) | copy-start | bytes 344068
  9.8 2.8 %copy-start.3 = (s32[112,256]{1,0:T(8,128)}, s32[112,256]{1,0:T(8,128)S(1)}, u32[]{:S(2)}) copy-start(s32[112,256]{1,0:T(8,128)S(1)} %collective-permute-done.1.c2) | copy-start | bytes 344068
  12.0 0.7 copy-start.4
  30.3 4.2 %copy-start.1 = (f32[64,2,32,128]{3,2,1,0:T(8,128)S(1)}, f32[64,2,32,128]{3,2,1,0:T(8,128)}, u32[]{:S(2)}) copy-start(f32[64,2,32,128]{3,2,1,0:T(8,128)} %shard_map.55) | copy-start | bytes 6291460
  31.7 2.7 %collective-permute-start.3 = (f32[32,2,32,128]{3,2,1,0:T(8,128)S(1)}, f32[32,2,32,128]{3,2,1,0:T(8,128)S(1)}, u32[]{:S(2)}, u32[]{:S(2)}) collective-permute-start(f32[32,2,32,128]{3,2,1,0:T(8,128)S(1)} %slice.41), channel_id=1, source_target_pairs={{0,1},{1,0},{2,3},{3,2},{4,5},{5,4},{6,7},{7,6},{8,9},{9,8},{10,11... | collective-permute-start | bytes 3145736 | tf_op jit(solution)/shard_map/ppermute | solution.py:260
  34.8 7.7 %collective-permute-start.4 = (f32[8,2,32,128]{3,2,1,0:T(8,128)S(1)}, f32[8,2,32,128]{3,2,1,0:T(8,128)S(1)}, u32[]{:S(2)}, u32[]{:S(2)}) collective-permute-start(f32[8,2,32,128]{3,2,1,0:T(8,128)S(1)} %get-tuple-element.5), channel_id=1, source_target_pairs={{0,8},{1,3},{2,10},{3,5},{4,12},{5,7},{6,14},{7,1},{8,16},{9,11},{... | collective-permute-start | bytes 786440 | tf_op jit(solution)/shard_map/ppermute | solution.py:263
  36.4 9.9 %collective-permute-start.5 = (f32[8,2,32,128]{3,2,1,0:T(8,128)S(1)}, f32[8,2,32,128]{3,2,1,0:T(8,128)S(1)}, u32[]{:S(2)}, u32[]{:S(2)}) collective-permute-start(f32[8,2,32,128]{3,2,1,0:T(8,128)S(1)} %get-tuple-element.7), channel_id=1, source_target_pairs={{0,16},{1,5},{2,18},{3,7},{4,20},{5,1},{6,22},{7,3},{8,24},{9,13},... | collective-permute-start | bytes 786440 | tf_op jit(solution)/shard_map/ppermute | solution.py:263
  39.2 7.2 %collective-permute-start.6 = (f32[8,2,32,128]{3,2,1,0:T(8,128)S(1)}, f32[8,2,32,128]{3,2,1,0:T(8,128)S(1)}, u32[]{:S(2)}, u32[]{:S(2)}) collective-permute-start(f32[8,2,32,128]{3,2,1,0:T(8,128)S(1)} %get-tuple-element.6), channel_id=1, source_target_pairs={{0,24},{1,7},{2,26},{3,1},{4,28},{5,3},{6,30},{7,5},{8,0},{9,15},{... | collective-permute-start | bytes 786440 | tf_op jit(solution)/shard_map/ppermute | solution.py:263
  46.4 5.9 %collective-permute-start.7 = (f32[2,2,32,128]{3,2,1,0:T(8,128)S(1)}, f32[2,2,32,128]{3,2,1,0:T(8,128)S(1)}, u32[]{:S(2)}, u32[]{:S(2)}) collective-permute-start(f32[2,2,32,128]{3,2,1,0:T(8,128)S(1)} %get-tuple-element.8), channel_id=1, source_target_pairs={{0,2},{1,9},{2,4},{3,11},{4,6},{5,13},{6,0},{7,15},{8,10},{9,17},{... | collective-permute-start | bytes 196616 | tf_op jit(solution)/shard_map/ppermute | solution.py:263
  48.1 5.8 %collective-permute-start.8 = (f32[2,2,32,128]{3,2,1,0:T(8,128)S(1)}, f32[2,2,32,128]{3,2,1,0:T(8,128)S(1)}, u32[]{:S(2)}, u32[]{:S(2)}) collective-permute-start(f32[2,2,32,128]{3,2,1,0:T(8,128)S(1)} %get-tuple-element.10), channel_id=1, source_target_pairs={{0,4},{1,17},{2,6},{3,19},{4,0},{5,21},{6,2},{7,23},{8,12},{9,25},... | collective-permute-start | bytes 196616 | tf_op jit(solution)/shard_map/ppermute | solution.py:263
  51.0 4.3 %collective-permute-start.9 = (f32[2,2,32,128]{3,2,1,0:T(8,128)S(1)}, f32[2,2,32,128]{3,2,1,0:T(8,128)S(1)}, u32[]{:S(2)}, u32[]{:S(2)}) collective-permute-start(f32[2,2,32,128]{3,2,1,0:T(8,128)S(1)} %get-tuple-element.9), channel_id=1, source_target_pairs={{0,6},{1,25},{2,0},{3,27},{4,2},{5,29},{6,4},{7,31},{8,14},{9,1},{... | collective-permute-start | bytes 196616 | tf_op jit(solution)/shard_map/ppermute | solution.py:263
  55.3 10.7 %collective-permute-start.10 = (f32[2,32,128]{2,1,0:T(8,128)S(1)}, f32[2,32,128]{2,1,0:T(8,128)S(1)}, u32[]{:S(2)}, u32[]{:S(2)}) collective-permute-start(f32[2,32,128]{2,1,0:T(8,128)S(1)} %get-tuple-element.16), channel_id=1, source_target_pairs={{0,0},{1,1},{2,2},{3,3},{4,4},{5,5},{6,6},{7,7},{8,8},{9,9},{10,10... | collective-permute-start | bytes 98312 | tf_op jit(solution)/shard_map/ppermute | solution.py:266
  60.2 9.4 %collective-permute-start.11 = (f32[2,32,128]{2,1,0:T(8,128)S(1)}, f32[2,32,128]{2,1,0:T(8,128)S(1)}, u32[]{:S(2)}, u32[]{:S(2)}) collective-permute-start(f32[2,32,128]{2,1,0:T(8,128)S(1)} %get-tuple-element.15), channel_id=1, source_target_pairs={{0,128},{1,129},{2,130},{3,131},{4,132},{5,133},{6,134},{7,135},{8... | collective-permute-start | bytes 98312 | tf_op jit(solution)/shard_map/ppermute | solution.py:266

commit v2 on v1

v2 whole, which is shorter than its diff:
```python
import functools
import jax
import jax.numpy as jnp
from jax import lax
from jax.experimental import pallas as pl
from jax.experimental.pallas import tpu as pltpu
from jax.sharding import PartitionSpec as P

AXES = ("depth", "freq")
H = 8
K = 6
Z = 4
NX = 256
NY = 256
CHUNK = 64
WIN = 112
HALO = 24
STEPS = WIN // 8
PAD = 8
ROWS = WIN + 2 * PAD
COMBINE = 7
IMAGE = 4
SKEW = 3
COMPS = 2
LIMIT = 32
LANES = 128
HALVES = NY // LANES


def split(linear):
    d, f = divmod(linear, 64)
    return d, f >> 5, (f >> 3) & 3, (f >> 1) & 3, f & 1


def join(d, zh, x, y, c):
    return d * 64 + ((zh * 4 + x) * 4 + y) * 2 + c


def route(move):
    return [(i, join(*move(*split(i)))) for i in range(256)]


def along_z(step):
    def move(d, zh, x, y, c):
        z = (zh * 4 + d + step(c)) % 8
        return z & 3, z >> 2, x, y, c

    return route(move)


def first_axis(t):
    def move(d, zh, x, y, c):
        return (d, zh, (x + t) % 4, y, c) if c == 0 else (d, zh, x, (y + t) % 4, c)

    return route(move)


def second_axis(t):
    def move(d, zh, x, y, c):
        return (d, zh, x, (y + t) % 4, c) if c == 0 else (d, zh, (x + t) % 4, y, c)

    return route(move)


def to_owner(p):
    def move(q, zh, x, y, c):
        far = (x >> 1) ^ (q & 1)
        return 2 * (p ^ zh) + (x >> 1), q >> 1, 2 * (q & 1) + ((x & 1) ^ far), y, c

    return route(move)


CORE_SWAP = route(lambda d, zh, x, y, c: (d, zh, x, y, 1 - c))


def window_start(q):
    return jnp.clip(CHUNK * q - HALO, 0, NX - WIN)


def lanes_of(shape=(8, LANES)):
    return lax.broadcasted_iota(jnp.int32, shape, 1)


def pick(v, ids, axis=1):
    return jnp.take_along_axis(v, ids, axis=axis, mode="promise_in_bounds")


def by_parity(lo, hi):
    lane = lanes_of()
    even = (2 * lane) & (LANES - 1)
    low = lane < LANES // 2
    return tuple(jnp.where(low, pick(lo, even + p), pick(hi, even + p)) for p in (0, 1))


def by_column(even, odd):
    lane = lanes_of()
    is_odd = (lane & 1) == 1
    return tuple(
        jnp.where(is_odd, pick(odd, (lane >> 1) + base), pick(even, (lane >> 1) + base)) for base in (0, LANES // 2)
    )


def cut_windows(place, classes, own, two, up, down, raw, parted, sem):
    quarter = NX // 4
    loads = []
    for n in range(4):
        rows = pl.ds(quarter * n, quarter)
        cp = pltpu.make_async_copy(classes.at[0, rows, :], raw.at[rows, :], sem.at[n])
        cp.start()
        loads.append(cp)
    for n in range(4):
        loads[n].wait()
        for r in range(quarter * n, quarter * (n + 1), 8):
            for half, v in enumerate(by_parity(raw[r : r + 8, 0:LANES], raw[r : r + 8, LANES:NY])):
                parted[half, r : r + 8, :] = v
    for n, ref in enumerate((own, two, up, down)):
        start = pl.multiple_of(place[4 + n], 8)
        for half in range(HALVES):
            for tile in range(STEPS):
                ref[half, 8 * tile : 8 * tile + 8, :] = parted[half, pl.ds(start + 8 * tile, 8), :]


def stencil(field, comp):
    lane = lanes_of()
    first_lane, last_lane = lane == 0, lane == LANES - 1
    for step in range(STEPS + SKEW * (K - 2)):
        for k in range(1, K):
            tile = step - SKEW * (k - 1)
            if not 0 <= tile < STEPS:
                continue
            r = PAD + 8 * tile
            g, rest = [], []
            for half in range(HALVES):
                v = field[k - 1, comp, half, r : r + 8, :]
                h = 0.5 * (field[k - 1, comp, half, r - 1 : r + 7, :] + field[k - 1, comp, half, r + 1 : r + 9, :])
                g.append(h + v)
                rest.append(h - v)
            before = jnp.where(first_lane, 0.0, pltpu.roll(g[1], 1, 1))
            after = jnp.where(last_lane, 0.0, pltpu.roll(g[0], LANES - 1, 1))
            sides = (before + g[1], g[0] + after)
            for half in range(HALVES):
                w = 0.5 * sides[half] + rest[half]
                if k == 1:
                    w = 0.5 * w
                else:
                    w = w - field[k - 2, comp, half, r : r + 8, :]
                field[k, comp, half, r : r + 8, :] = w


def stencils(field):
    def some(step, carry):
        for part in range(COMPS):
            stencil(field, COMPS * step + part)
        return carry

    lax.fori_loop(0, 4 // COMPS, some, 0)


def clear_ends(field):
    zero = jnp.zeros((8, LANES), jnp.float32)
    for k in range(K - 1):
        for comp in range(4):
            for half in range(HALVES):
                field[k, comp, half, 0:PAD, :] = zero
                field[k, comp, half, PAD + WIN : ROWS, :] = zero


def first_terms(place, src, rec, field, raw, sem):
    start = pl.multiple_of(place[4], 8)
    loads = []
    for n, ref in enumerate((src, rec)):
        cp = pltpu.make_async_copy(ref.at[0, :, pl.ds(start, WIN), :], raw.at[n], sem.at[n])
        cp.start()
        loads.append(cp)
    clear_ends(field)
    for n in range(2):
        loads[n].wait()
        for part in range(2):
            for tile in range(STEPS):
                r = 8 * tile
                lo, hi = raw[n, part, r : r + 8, 0:LANES], raw[n, part, r : r + 8, LANES:NY]
                for half, v in enumerate(by_parity(lo, hi)):
                    field[0, 2 * n + part, half, PAD + r : PAD + r + 8, :] = v
    stencils(field)


def all_levels(place, first, w0, w1, w2, w3, coef, keep, send, field, cls, table):
    q, x_at, y_at, core = place[0], place[1], place[2], place[3]
    for n, ref in enumerate((w0, w1, w2, w3)):
        level = place[8 + n]
        for half in range(HALVES):
            for tile in range(STEPS):
                cls[level, half, 8 * tile : 8 * tile + 8, :] = ref[half, 8 * tile : 8 * tile + 8, :]
    clear_ends(field)
    for n in range(2 * K):
        table[n] = jnp.broadcast_to(coef[n : n + 1, :], (8, LANES))
    mirror = 7 - lax.broadcasted_iota(jnp.int32, (8, LANES), 0)
    base = pl.multiple_of(PAD + CHUNK * q - place[4], 8)

    def finish(level, terms):
        def combine(step, carry):
            places = []
            for part in range(COMBINE):
                r = pl.multiple_of(PAD + 8 * (COMBINE * step + part), 8)
                places += [(half, r) for half in range(HALVES)]

            def look_up(half, r):
                ids = cls[level, half, pl.ds(r - PAD, 8), :]
                return [pick(table[n], ids) for n in range(2 * K)]

            ahead = look_up(*places[0])
            for n, (half, r) in enumerate(places):
                coefs = ahead
                if n + 1 < len(places):
                    ahead = look_up(*places[n + 1])
                p, s = [], []
                for comp in range(4):
                    vals = [terms[k, comp, half, pl.ds(r, 8), :] for k in range(K)]
                    a, b = coefs[0] * vals[0], coefs[K] * vals[0]
                    for k in range(1, K):
                        a = a + coefs[k] * vals[k]
                        b = b + coefs[K + k] * vals[k]
                    p.append(a)
                    s.append(b)
                field[0, 0, half, pl.ds(r, 8), :] = p[0] + s[1]
                field[0, 1, half, pl.ds(r, 8), :] = p[1] - s[0]
                field[0, 2, half, pl.ds(r, 8), :] = p[2] - s[3]
                field[0, 3, half, pl.ds(r, 8), :] = p[3] + s[2]
            return carry

        lax.fori_loop(0, STEPS // COMBINE, combine, 0)
        lb, e = level >> 1, level & 1

        def image(step, carry):
            for part in range(IMAGE):
                image_rows(IMAGE * step + part)
            return carry

        def image_rows(m):
            y_o, ix = m & 3, m >> 2
            x_o = 2 * e + (ix ^ e ^ (q & 1))
            dx, dy = (x_o - x_at) & 3, (y_o - y_at) & 3
            for flip, ref in enumerate((keep, send)):
                c_o = core ^ flip
                t = jnp.where(c_o == 0, dx, dy)
                u = jnp.where(c_o == 0, dy, dx)
                at = (t * 4 + u) * 2 + lb
                for row in range(4):
                    x = base + 4 * (2 * m + c_o) + row
                    for half in range(HALVES):
                        s_re, s_im = [pick(field[0, comp, half, pl.ds(x - 3, 8), :], mirror, 0) for comp in (0, 1)]
                        r_re, r_im = [field[0, comp, half, pl.ds(x - 4, 8), :] for comp in (2, 3)]
                        ref[at, half, H * row : H * row + H, :] = s_re * r_re + s_im * r_im

        lax.fori_loop(0, 8 // IMAGE, image, 0)

    finish(0, first)

    def level_body(level, carry):
        stencils(field)
        finish(level, field)
        return carry

    lax.fori_loop(1, Z, level_body, 0)


def last_sum(a, b, out):
    scaling = 64.0 ** -0.5
    for tile in range(4):
        rows = slice(8 * tile, 8 * tile + 8)
        parts = [(a[half, rows, :] + b[half, rows, :]) * scaling for half in range(HALVES)]
        lo, hi = by_column(*parts)
        out[tile, 0, :, 0:LANES] = lo
        out[tile, 0, :, LANES:NY] = hi


SCALARS = pl.BlockSpec(memory_space=pltpu.SMEM)
LOCAL = pl.BlockSpec(memory_space=pltpu.VMEM)
REMOTE = pl.BlockSpec(memory_space=pltpu.HBM)
TERMS = (K, 4, HALVES, ROWS, LANES)
WINDOW = (HALVES, WIN, LANES)


def call(body, outs, ins, scratch=(), flops=0, moved=0):
    return pl.pallas_call(
        body,
        out_shape=[jax.ShapeDtypeStruct(shape, dtype) for shape, dtype in outs],
        in_specs=ins,
        out_specs=[LOCAL] * len(outs),
        scratch_shapes=list(scratch),
        cost_estimate=pl.CostEstimate(flops=flops, bytes_accessed=moved, transcendentals=0),
        compiler_params=pltpu.CompilerParams(vmem_limit_bytes=LIMIT * 2**20),
    )


def per_device(source, receiver, classes, coef_table, freq_list):
    q = lax.axis_index("depth")
    f = lax.axis_index("freq")
    zh, x_at, y_at, core = f >> 5, (f >> 3) & 3, (f >> 1) & 3, f & 1
    starts = [window_start((q + step) & 3) for step in (0, 2, 1, -1)]
    levels = [(q + step) & 3 for step in (0, 2, -1, 1)]
    place = jnp.stack([q, x_at, y_at, core] + starts + levels).astype(jnp.int32)
    own, two, up, down = call(
        cut_windows,
        [(WINDOW, jnp.int32)] * 4,
        [SCALARS, REMOTE],
        [pltpu.VMEM((NX, NY), jnp.int32), pltpu.VMEM((HALVES, NX, LANES), jnp.int32), pltpu.SemaphoreType.DMA((4,))],
    )(place, classes)
    class_windows = [
        own,
        lax.ppermute(two, AXES, along_z(lambda c: 2 if c == 0 else -2)),
        lax.ppermute(up, AXES, along_z(lambda c: 1)),
        lax.ppermute(down, AXES, along_z(lambda c: -1)),
    ]
    mine = lax.dynamic_slice_in_dim(coef_table, freq_list[0], 1, axis=1)[:, 0]
    rows = jnp.transpose(mine, (1, 2, 0)).reshape(2 * K, -1)
    coef = jnp.pad(rows, [(0, 4), (0, LANES - rows.shape[1])])
    (first,) = call(
        first_terms,
        [(TERMS, jnp.float32)],
        [SCALARS, REMOTE, REMOTE],
        [pltpu.VMEM((2, 2, WIN, NY), jnp.float32), pltpu.SemaphoreType.DMA((2,))],
        flops=10**7,
        moved=4 * 2**20,
    )(place, source, receiver)
    half_image = ((32, HALVES, 4 * H, LANES), jnp.float32)
    keep, send = call(
        all_levels,
        [half_image, half_image],
        [SCALARS] + [LOCAL] * 6,
        [
            pltpu.VMEM(TERMS, jnp.float32),
            pltpu.VMEM((Z,) + WINDOW, jnp.int32),
            pltpu.VMEM((2 * K, 8, LANES), jnp.float32),
        ],
        flops=5 * 10**7,
        moved=4 * 2**20,
    )(place, first, *class_windows, coef)

    mine = keep + lax.ppermute(send, AXES, CORE_SWAP)
    for axis in (first_axis, second_axis):
        part = mine.shape[0] // 4
        got = [lax.ppermute(mine[t * part : (t + 1) * part], AXES, axis(t)) for t in (1, 2, 3)]
        mine = mine[:part] + got[0] + got[1] + got[2]
    sent = [lax.dynamic_index_in_dim(mine, p ^ zh, 0, keepdims=False) for p in (0, 1)]
    got = [lax.ppermute(sent[p], AXES, to_owner(p)) for p in (0, 1)]
    (image,) = call(last_sum, [((4, 1, H, NY), jnp.float32)], [LOCAL, LOCAL])(*got)
    return image


def solution(mesh):
    placed = (
        P("freq", None, None, None),
        P("freq", None, None, None),
        P("depth", None, None),
        P(),
        P("freq"),
    )
    return jax.shard_map(
        per_device,
        mesh=mesh,
        in_specs=placed,
        out_specs=P("freq", "depth", None, None),
        check_vma=False,
    )
```

time: 71.5 us -> 61.5 us (0.86); the launches traced: 70.2 us -> 61.2 us
  Pallas kernels: 17.6 us -> 12.5 us
  starting transfers between devices: 29 us -> 26.2 us
  local copies, waits for them, and re-layouts: 4.94 us -> 3.54 us
  waiting for transfers between devices: 16.9 us -> 17.8 us
    pallas_call x1 -> x4, Pallas kernels: 17.6 us -> 12.5 us  [the longest x1 7.59 us: per_device(): call(all_levels, [half_image, half_image], [SCALARS] + [LOCAL] * 6, [pltp...]
    unnamed x10 -> x8, local copies, waits for them, and re-layouts: 0.02 us -> 3.03 us
    ppermute x6, starting transfers between devices: 17.3 us -> 14.6 us  [the longest x2 8.04 us: per_device(): got = [lax.ppermute(sent[p], AXES, to_owner(p)) for p in (0, 1)]]
    dynamic_slice x1 -> x0, local copies, waits for them, and re-layouts: 1.79 us -> none  [window(): lax.dynamic_slice(classes[0], (window_start(target & 3), 0), (WIN, NY))]
    slice x1 -> x0, local copies, waits for them, and re-layouts: 1.45 us -> none  [per_device(): mine = terms[:32] + lax.ppermute(terms[32:], AXES, CORE_SWAP)]
    ppermute x6, waiting for transfers between devices: 8.26 us -> 9.14 us  [the longest x2 6.49 us: per_device(): got = [lax.ppermute(sent[p], AXES, to_owner(p)) for p in (0, 1)]]
  transfers between devices with their start and end apart: 12 -> 12, of which waited for: 7 -> 6; matrix products, arithmetic and copies ran while one was open for 1% -> 1% of each run, Pallas kernels for 0% -> 4%
where the time goes in v2:
time: 61.5 us; the launch traced here: 61.2 us
  starting transfers between devices  26.2 us (43%)
  waiting for transfers between devices  17.8 us (29%)
  Pallas kernels  12.5 us (20%)
  local copies, waits for them, and re-layouts  3.54 us (6%)
  between operations  0.81 us (1%)
    ppermute x6, starting transfers between devices, per_device(): lax.ppermute(mine[t * part:(t + 1) * part], AXES, axis(t))  11.6 us
    ppermute x6, waiting for transfers between devices, per_device(): lax.ppermute(mine[t * part:(t + 1) * part], AXES, axis(t))  8.64 us
    ppermute x2, starting transfers between devices, per_device(): got = [lax.ppermute(sent[p], AXES, to_owner(p)) for p in (0, 1)]  8.04 us
    pallas_call x1, Pallas kernels, per_device(): call(all_levels, [half_image, half_image], [SCALARS] + [LOCAL] * 6, [pltp...  7.59 us
    ppermute x2, waiting for transfers between devices, per_device(): got = [lax.ppermute(sent[p], AXES, to_owner(p)) for p in (0, 1)]  6.49 us
    ppermute x1, starting transfers between devices, per_device(): lax.ppermute(two, AXES, along_z(lambda c: 2 if c == 0 else -2))  3.35 us
    ppermute x1, starting transfers between devices, per_device(): lax.ppermute(up, AXES, along_z(lambda c: 1))  3.13 us
    unnamed x8, local copies, waits for them, and re-layouts  3.03 us
  transfers between devices with their start and end apart: 12, of which 6 were waited for; matrix products, arithmetic and copies ran while one was open for 1% of the time, Pallas kernels for 4%

profile of v2, /device:TPU:32, one launch (start us, length us, event | category | flops | bytes accessed | tf_op | source)
XLA Modules:
  0.0 61.2 jit_solution(15162200977831830158)
XLA Ops:
  0.0 0.0 copy-start
  0.0 0.1 stack.51.place
  0.1 0.0 copy-start.3
  0.1 0.9 %copy-done.3 = s32[1,256,256]{2,1,0:T(8,128)S(1)} copy-done((s32[1,256,256]{2,1,0:T(8,128)S(1)}, s32[1,256,256]{2,1,0:T(8,128)}, u32[]{:S(2)}) %copy-start.3) | copy-done | bytes 262168
  1.0 1.5 %shard_map.56 = (s32[2,112,128]{2,1,0:T(8,128)S(1)}, s32[2,112,128]{2,1,0:T(8,128)S(1)}, s32[2,112,128]{2,1,0:T(8,128)S(1)}, s32[2,112,128]{2,1,0:T(8,128)S(1)}) custom-call(s32[12]{0:T(128)S(1)} %stack.51.place, s32[1,256,256]{2,1,0:T(8,128)S(1)} %copy-done.3), custom_call_target="tpu_custom_call" | custom-call | tf_op jit(solution)/shard_map/pallas_call | solution.py:303
  2.6 3.3 %collective-permute-start = (s32[2,112,128]{2,1,0:T(8,128)S(1)}, s32[2,112,128]{2,1,0:T(8,128)S(1)}, u32[]{:S(2)}, u32[]{:S(2)}) collective-permute-start(s32[2,112,128]{2,1,0:T(8,128)S(1)} %get-tuple-element.12), channel_id=1, source_target_pairs={{0,128},{1,161},{2,130},{3,163},{4,132},{5,165},{6,134},{7,167},{8... | collective-permute-start | bytes 344072 | tf_op jit(solution)/shard_map/ppermute | solution.py:311
  5.9 3.1 %collective-permute-start.1 = (s32[2,112,128]{2,1,0:T(8,128)S(1)}, s32[2,112,128]{2,1,0:T(8,128)S(1)}, u32[]{:S(2)}, u32[]{:S(2)}) collective-permute-start(s32[2,112,128]{2,1,0:T(8,128)S(1)} %get-tuple-element.13), channel_id=1, source_target_pairs={{0,64},{1,65},{2,66},{3,67},{4,68},{5,69},{6,70},{7,71},{8,72},{9,... | collective-permute-start | bytes 344072 | tf_op jit(solution)/shard_map/ppermute | solution.py:312
  9.0 0.0 collective-permute-start.2
  9.7 0.0 copy-done
  9.7 0.2 constant_dynamic-slice_fusion
  9.9 0.1 copy.6
  10.0 0.0 copy-start.1
  10.1 1.0 %copy-done.1 = f32[1,2,256,256]{3,2,1,0:T(8,128)S(1)} copy-done((f32[1,2,256,256]{3,2,1,0:T(8,128)S(1)}, f32[1,2,256,256]{3,2,1,0:T(8,128)}, u32[]{:S(2)}) %copy-start.1) | copy-done | bytes 524312
  11.1 0.0 copy-start.2
  11.1 1.0 %copy-done.2 = f32[1,2,256,256]{3,2,1,0:T(8,128)S(1)} copy-done((f32[1,2,256,256]{3,2,1,0:T(8,128)S(1)}, f32[1,2,256,256]{3,2,1,0:T(8,128)}, u32[]{:S(2)}) %copy-start.2) | copy-done | bytes 524312
  12.1 2.7 %shard_map.55.first = f32[6,4,2,128,128]{4,3,2,1,0:T(8,128)S(1)} custom-call(s32[12]{0:T(128)S(1)} %stack.51.place, f32[1,2,256,256]{3,2,1,0:T(8,128)S(1)} %copy-done.1, f32[1,2,256,256]{3,2,1,0:T(8,128)S(1)} %copy-done.2), custom_call_target="tpu_custom_call" | custom-call | flops 10000000 | bytes 4194304 | tf_op jit(solution)/shard_map/pallas_call | solution.py:318
  14.9 0.0 collective-permute-done.w1
  14.9 0.0 collective-permute-done.1.w2
  14.9 0.0 collective-permute-done.2.w3
  14.9 7.6 %shard_map.57 = (f32[32,2,32,128]{3,2,1,0:T(8,128)S(1)}, f32[32,2,32,128]{3,2,1,0:T(8,128)S(1)}) custom-call(s32[12]{0:T(128)S(1)} %stack.51.place, f32[6,4,2,128,128]{4,3,2,1,0:T(8,128)S(1)} %shard_map.55.first, s32[2,112,128]{2,1,0:T(8,128)S(1)} %get-tuple-element.11.w0, s32[2,112,128]{2,1,0:T(8,128)S(1)} %collective-permute-done.w1, ...), custom_call_target="tpu_custom_call" | custom-call | flops 50000000 | bytes 4194304 | tf_op jit(solution)/shard_map/pallas_call | solution.py:327
  22.5 0.1 collective-permute-start.3
  22.6 2.6 %collective-permute-done.3 = f32[32,2,32,128]{3,2,1,0:T(8,128)S(1)} collective-permute-done((f32[32,2,32,128]{3,2,1,0:T(8,128)S(1)}, f32[32,2,32,128]{3,2,1,0:T(8,128)S(1)}, u32[]{:S(2)}, u32[]{:S(2)}) %collective-permute-start.3) | collective-permute-done | bytes 1048608 | tf_op jit(solution)/shard_map/ppermute | solution.py:340
  25.3 0.2 add.53
  25.5 0.1 fusion.4
  25.5 1.6 %collective-permute-start.4 = (f32[8,2,32,128]{3,2,1,0:T(8,128)S(1)}, f32[8,2,32,128]{3,2,1,0:T(8,128)S(1)}, u32[]{:S(2)}, u32[]{:S(2)}) collective-permute-start(f32[8,2,32,128]{3,2,1,0:T(8,128)S(1)} %get-tuple-element.17), channel_id=1, source_target_pairs={{0,8},{1,3},{2,10},{3,5},{4,12},{5,7},{6,14},{7,1},{8,16},{9,11},{... | collective-permute-start | bytes 786440 | tf_op jit(solution)/shard_map/ppermute | solution.py:343
  27.1 2.7 %collective-permute-start.5 = (f32[8,2,32,128]{3,2,1,0:T(8,128)S(1)}, f32[8,2,32,128]{3,2,1,0:T(8,128)S(1)}, u32[]{:S(2)}, u32[]{:S(2)}) collective-permute-start(f32[8,2,32,128]{3,2,1,0:T(8,128)S(1)} %get-tuple-element.19), channel_id=1, source_target_pairs={{0,16},{1,5},{2,18},{3,7},{4,20},{5,1},{6,22},{7,3},{8,24},{9,13},... | collective-permute-start | bytes 786440 | tf_op jit(solution)/shard_map/ppermute | solution.py:343
  29.8 1.4 %collective-permute-start.6 = (f32[8,2,32,128]{3,2,1,0:T(8,128)S(1)}, f32[8,2,32,128]{3,2,1,0:T(8,128)S(1)}, u32[]{:S(2)}, u32[]{:S(2)}) collective-permute-start(f32[8,2,32,128]{3,2,1,0:T(8,128)S(1)} %get-tuple-element.18), channel_id=1, source_target_pairs={{0,24},{1,7},{2,26},{3,1},{4,28},{5,3},{6,30},{7,5},{8,0},{9,15},{... | collective-permute-start | bytes 786440 | tf_op jit(solution)/shard_map/ppermute | solution.py:343
  31.3 1.9 %collective-permute-done.4 = f32[8,2,32,128]{3,2,1,0:T(8,128)S(1)} collective-permute-done((f32[8,2,32,128]{3,2,1,0:T(8,128)S(1)}, f32[8,2,32,128]{3,2,1,0:T(8,128)S(1)}, u32[]{:S(2)}, u32[]{:S(2)}) %collective-permute-start.4) | collective-permute-done | bytes 262176 | tf_op jit(solution)/shard_map/ppermute | solution.py:343
  33.2 3.8 %collective-permute-done.5 = f32[8,2,32,128]{3,2,1,0:T(8,128)S(1)} collective-permute-done((f32[8,2,32,128]{3,2,1,0:T(8,128)S(1)}, f32[8,2,32,128]{3,2,1,0:T(8,128)S(1)}, u32[]{:S(2)}, u32[]{:S(2)}) %collective-permute-start.5) | collective-permute-done | bytes 262176 | tf_op jit(solution)/shard_map/ppermute | solution.py:343
  37.0 0.0 collective-permute-done.6
  37.0 0.1 fusion.1
  37.1 1.7 %collective-permute-start.7 = (f32[2,2,32,128]{3,2,1,0:T(8,128)S(1)}, f32[2,2,32,128]{3,2,1,0:T(8,128)S(1)}, u32[]{:S(2)}, u32[]{:S(2)}) collective-permute-start(f32[2,2,32,128]{3,2,1,0:T(8,128)S(1)} %get-tuple-element.20), channel_id=1, source_target_pairs={{0,2},{1,9},{2,4},{3,11},{4,6},{5,13},{6,0},{7,15},{8,10},{9,17},{... | collective-permute-start | bytes 196616 | tf_op jit(solution)/shard_map/ppermute | solution.py:343
  38.8 2.9 %collective-permute-start.8 = (f32[2,2,32,128]{3,2,1,0:T(8,128)S(1)}, f32[2,2,32,128]{3,2,1,0:T(8,128)S(1)}, u32[]{:S(2)}, u32[]{:S(2)}) collective-permute-start(f32[2,2,32,128]{3,2,1,0:T(8,128)S(1)} %get-tuple-element.22), channel_id=1, source_target_pairs={{0,4},{1,17},{2,6},{3,19},{4,0},{5,21},{6,2},{7,23},{8,12},{9,25},... | collective-permute-start | bytes 196616 | tf_op jit(solution)/shard_map/ppermute | solution.py:343
  41.7 1.3 %collective-permute-start.9 = (f32[2,2,32,128]{3,2,1,0:T(8,128)S(1)}, f32[2,2,32,128]{3,2,1,0:T(8,128)S(1)}, u32[]{:S(2)}, u32[]{:S(2)}) collective-permute-start(f32[2,2,32,128]{3,2,1,0:T(8,128)S(1)} %get-tuple-element.21), channel_id=1, source_target_pairs={{0,6},{1,25},{2,0},{3,27},{4,2},{5,29},{6,4},{7,31},{8,14},{9,1},{... | collective-permute-start | bytes 196616 | tf_op jit(solution)/shard_map/ppermute | solution.py:343
  43.0 0.0 collective-permute-done.7
  43.0 1.6 %collective-permute-done.8 = f32[2,2,32,128]{3,2,1,0:T(8,128)S(1)} collective-permute-done((f32[2,2,32,128]{3,2,1,0:T(8,128)S(1)}, f32[2,2,32,128]{3,2,1,0:T(8,128)S(1)}, u32[]{:S(2)}, u32[]{:S(2)}) %collective-permute-start.8) | collective-permute-done | bytes 65568 | tf_op jit(solution)/shard_map/ppermute | solution.py:343
  44.6 1.3 %collective-permute-done.9 = f32[2,2,32,128]{3,2,1,0:T(8,128)S(1)} collective-permute-done((f32[2,2,32,128]{3,2,1,0:T(8,128)S(1)}, f32[2,2,32,128]{3,2,1,0:T(8,128)S(1)}, u32[]{:S(2)}, u32[]{:S(2)}) %collective-permute-start.9) | collective-permute-done | bytes 65568 | tf_op jit(solution)/shard_map/ppermute | solution.py:343
  46.0 5.4 %collective-permute-start.10 = (f32[2,32,128]{2,1,0:T(8,128)S(1)}, f32[2,32,128]{2,1,0:T(8,128)S(1)}, u32[]{:S(2)}, u32[]{:S(2)}) collective-permute-start(f32[2,32,128]{2,1,0:T(8,128)S(1)} %get-tuple-element.24), channel_id=1, source_target_pairs={{0,0},{1,1},{2,2},{3,3},{4,4},{5,5},{6,6},{7,7},{8,8},{9,9},{10,10... | collective-permute-start | bytes 98312 | tf_op jit(solution)/shard_map/ppermute | solution.py:346
  51.4 2.6 %collective-permute-start.11 = (f32[2,32,128]{2,1,0:T(8,128)S(1)}, f32[2,32,128]{2,1,0:T(8,128)S(1)}, u32[]{:S(2)}, u32[]{:S(2)}) collective-permute-start(f32[2,32,128]{2,1,0:T(8,128)S(1)} %get-tuple-element.23), channel_id=1, source_target_pairs={{0,128},{1,129},{2,130},{3,131},{4,132},{5,133},{6,134},{7,135},{8... | collective-permute-start | bytes 98312 | tf_op jit(solution)/shard_map/ppermute | solution.py:346
  54.0 0.0 collective-permute-done.10.a
  54.0 6.5 %collective-permute-done.11.b = f32[2,32,128]{2,1,0:T(8,128)S(1)} collective-permute-done((f32[2,32,128]{2,1,0:T(8,128)S(1)}, f32[2,32,128]{2,1,0:T(8,128)S(1)}, u32[]{:S(2)}, u32[]{:S(2)}) %collective-permute-start.11) | collective-permute-done | bytes 32800 | tf_op jit(solution)/shard_map/ppermute | solution.py:346
  60.5 0.7 %shard_map.58 = f32[4,1,8,256]{3,2,1,0:T(8,128)} custom-call(f32[2,32,128]{2,1,0:T(8,128)S(1)} %collective-permute-done.10.a, f32[2,32,128]{2,1,0:T(8,128)S(1)} %collective-permute-done.11.b), custom_call_target="tpu_custom_call" | custom-call | tf_op jit(solution)/shard_map/pallas_call | solution.py:347
  (6 shorter events, 0.1 us)
Async XLA Ops:
  0.0 9.7 %copy-start = (f32[16,64,2,6]{1,2,3,0:T(2,128)S(1)}, f32[16,64,2,6]{1,2,3,0:T(2,128)}, u32[]{:S(2)}) copy-start(f32[16,64,2,6]{1,2,3,0:T(2,128)} %param.8) | copy-start | bytes 147460
  0.1 1.0 %copy-start.3 = (s32[1,256,256]{2,1,0:T(8,128)S(1)}, s32[1,256,256]{2,1,0:T(8,128)}, u32[]{:S(2)}) copy-start(s32[1,256,256]{2,1,0:T(8,128)} %classes.1) | copy-start | bytes 786436
  2.6 12.3 %collective-permute-start = (s32[2,112,128]{2,1,0:T(8,128)S(1)}, s32[2,112,128]{2,1,0:T(8,128)S(1)}, u32[]{:S(2)}, u32[]{:S(2)}) collective-permute-start(s32[2,112,128]{2,1,0:T(8,128)S(1)} %get-tuple-element.12), channel_id=1, source_target_pairs={{0,128},{1,161},{2,130},{3,163},{4,132},{5,165},{6,134},{7,167},{8... | collective-permute-start | bytes 344072 | tf_op jit(solution)/shard_map/ppermute | solution.py:311
  5.9 9.0 %collective-permute-start.1 = (s32[2,112,128]{2,1,0:T(8,128)S(1)}, s32[2,112,128]{2,1,0:T(8,128)S(1)}, u32[]{:S(2)}, u32[]{:S(2)}) collective-permute-start(s32[2,112,128]{2,1,0:T(8,128)S(1)} %get-tuple-element.13), channel_id=1, source_target_pairs={{0,64},{1,65},{2,66},{3,67},{4,68},{5,69},{6,70},{7,71},{8,72},{9,... | collective-permute-start | bytes 344072 | tf_op jit(solution)/shard_map/ppermute | solution.py:312
  9.0 5.9 %collective-permute-start.2 = (s32[2,112,128]{2,1,0:T(8,128)S(1)}, s32[2,112,128]{2,1,0:T(8,128)S(1)}, u32[]{:S(2)}, u32[]{:S(2)}) collective-permute-start(s32[2,112,128]{2,1,0:T(8,128)S(1)} %get-tuple-element.14), channel_id=1, source_target_pairs={{0,224},{1,225},{2,226},{3,227},{4,228},{5,229},{6,230},{7,231},{8... | collective-permute-start | bytes 344072 | tf_op jit(solution)/shard_map/ppermute | solution.py:313
  10.0 1.0 %copy-start.1 = (f32[1,2,256,256]{3,2,1,0:T(8,128)S(1)}, f32[1,2,256,256]{3,2,1,0:T(8,128)}, u32[]{:S(2)}) copy-start(f32[1,2,256,256]{3,2,1,0:T(8,128)} %src.1) | copy-start | bytes 1572868
  11.1 1.0 %copy-start.2 = (f32[1,2,256,256]{3,2,1,0:T(8,128)S(1)}, f32[1,2,256,256]{3,2,1,0:T(8,128)}, u32[]{:S(2)}) copy-start(f32[1,2,256,256]{3,2,1,0:T(8,128)} %rec.1) | copy-start | bytes 1572868
  22.5 2.7 %collective-permute-start.3 = (f32[32,2,32,128]{3,2,1,0:T(8,128)S(1)}, f32[32,2,32,128]{3,2,1,0:T(8,128)S(1)}, u32[]{:S(2)}, u32[]{:S(2)}) collective-permute-start(f32[32,2,32,128]{3,2,1,0:T(8,128)S(1)} %get-tuple-element.16), channel_id=1, source_target_pairs={{0,1},{1,0},{2,3},{3,2},{4,5},{5,4},{6,7},{7,6},{8,9},{9,8},{10,11... | collective-permute-start | bytes 3145736 | tf_op jit(solution)/shard_map/ppermute | solution.py:340
  25.5 7.7 %collective-permute-start.4 = (f32[8,2,32,128]{3,2,1,0:T(8,128)S(1)}, f32[8,2,32,128]{3,2,1,0:T(8,128)S(1)}, u32[]{:S(2)}, u32[]{:S(2)}) collective-permute-start(f32[8,2,32,128]{3,2,1,0:T(8,128)S(1)} %get-tuple-element.17), channel_id=1, source_target_pairs={{0,8},{1,3},{2,10},{3,5},{4,12},{5,7},{6,14},{7,1},{8,16},{9,11},{... | collective-permute-start | bytes 786440 | tf_op jit(solution)/shard_map/ppermute | solution.py:343
  27.1 9.9 %collective-permute-start.5 = (f32[8,2,32,128]{3,2,1,0:T(8,128)S(1)}, f32[8,2,32,128]{3,2,1,0:T(8,128)S(1)}, u32[]{:S(2)}, u32[]{:S(2)}) collective-permute-start(f32[8,2,32,128]{3,2,1,0:T(8,128)S(1)} %get-tuple-element.19), channel_id=1, source_target_pairs={{0,16},{1,5},{2,18},{3,7},{4,20},{5,1},{6,22},{7,3},{8,24},{9,13},... | collective-permute-start | bytes 786440 | tf_op jit(solution)/shard_map/ppermute | solution.py:343
  29.8 7.2 %collective-permute-start.6 = (f32[8,2,32,128]{3,2,1,0:T(8,128)S(1)}, f32[8,2,32,128]{3,2,1,0:T(8,128)S(1)}, u32[]{:S(2)}, u32[]{:S(2)}) collective-permute-start(f32[8,2,32,128]{3,2,1,0:T(8,128)S(1)} %get-tuple-element.18), channel_id=1, source_target_pairs={{0,24},{1,7},{2,26},{3,1},{4,28},{5,3},{6,30},{7,5},{8,0},{9,15},{... | collective-permute-start | bytes 786440 | tf_op jit(solution)/shard_map/ppermute | solution.py:343
  37.1 5.9 %collective-permute-start.7 = (f32[2,2,32,128]{3,2,1,0:T(8,128)S(1)}, f32[2,2,32,128]{3,2,1,0:T(8,128)S(1)}, u32[]{:S(2)}, u32[]{:S(2)}) collective-permute-start(f32[2,2,32,128]{3,2,1,0:T(8,128)S(1)} %get-tuple-element.20), channel_id=1, source_target_pairs={{0,2},{1,9},{2,4},{3,11},{4,6},{5,13},{6,0},{7,15},{8,10},{9,17},{... | collective-permute-start | bytes 196616 | tf_op jit(solution)/shard_map/ppermute | solution.py:343
  38.8 5.8 %collective-permute-start.8 = (f32[2,2,32,128]{3,2,1,0:T(8,128)S(1)}, f32[2,2,32,128]{3,2,1,0:T(8,128)S(1)}, u32[]{:S(2)}, u32[]{:S(2)}) collective-permute-start(f32[2,2,32,128]{3,2,1,0:T(8,128)S(1)} %get-tuple-element.22), channel_id=1, source_target_pairs={{0,4},{1,17},{2,6},{3,19},{4,0},{5,21},{6,2},{7,23},{8,12},{9,25},... | collective-permute-start | bytes 196616 | tf_op jit(solution)/shard_map/ppermute | solution.py:343
  41.7 4.3 %collective-permute-start.9 = (f32[2,2,32,128]{3,2,1,0:T(8,128)S(1)}, f32[2,2,32,128]{3,2,1,0:T(8,128)S(1)}, u32[]{:S(2)}, u32[]{:S(2)}) collective-permute-start(f32[2,2,32,128]{3,2,1,0:T(8,128)S(1)} %get-tuple-element.21), channel_id=1, source_target_pairs={{0,6},{1,25},{2,0},{3,27},{4,2},{5,29},{6,4},{7,31},{8,14},{9,1},{... | collective-permute-start | bytes 196616 | tf_op jit(solution)/shard_map/ppermute | solution.py:343
  46.0 8.1 %collective-permute-start.10 = (f32[2,32,128]{2,1,0:T(8,128)S(1)}, f32[2,32,128]{2,1,0:T(8,128)S(1)}, u32[]{:S(2)}, u32[]{:S(2)}) collective-permute-start(f32[2,32,128]{2,1,0:T(8,128)S(1)} %get-tuple-element.24), channel_id=1, source_target_pairs={{0,0},{1,1},{2,2},{3,3},{4,4},{5,5},{6,6},{7,7},{8,8},{9,9},{10,10... | collective-permute-start | bytes 98312 | tf_op jit(solution)/shard_map/ppermute | solution.py:346
  51.4 9.1 %collective-permute-start.11 = (f32[2,32,128]{2,1,0:T(8,128)S(1)}, f32[2,32,128]{2,1,0:T(8,128)S(1)}, u32[]{:S(2)}, u32[]{:S(2)}) collective-permute-start(f32[2,32,128]{2,1,0:T(8,128)S(1)} %get-tuple-element.23), channel_id=1, source_target_pairs={{0,128},{1,129},{2,130},{3,131},{4,132},{5,133},{6,134},{7,135},{8... | collective-permute-start | bytes 98312 | tf_op jit(solution)/shard_map/ppermute | solution.py:346

commit v3 on v2

--- a/solution.py
+++ b/solution.py
@@ -62,10 +62,20 @@
     return route(move)
 
 
+def chunk_at(z):
+    return ((z & 3) + 2 * (z >> 2) + 3) & 3
+
+
+def sent_first(q, zh):
+    return 1 ^ zh ^ (q & 1) ^ (q >> 1)
+
+
 def to_owner(p):
-    def move(q, zh, x, y, c):
-        far = (x >> 1) ^ (q & 1)
-        return 2 * (p ^ zh) + (x >> 1), q >> 1, 2 * (q & 1) + ((x & 1) ^ far), y, c
+    def move(d, zh, x, y, c):
+        q = chunk_at(4 * zh + d)
+        e = (x >> 1) ^ (q & 1)
+        level = e ^ (3 * (p ^ sent_first(q, zh)))
+        return level, q >> 1, 2 * (q & 1) + ((x & 1) ^ e), y, c
 
     return route(move)
 
@@ -229,7 +239,8 @@
             return carry
 
         lax.fori_loop(0, STEPS // COMBINE, combine, 0)
-        lb, e = level >> 1, level & 1
+        lb = level >> 1
+        e = (level ^ lb) & 1
 
         def image(step, carry):
             for part in range(IMAGE):
@@ -238,7 +249,7 @@
 
         def image_rows(m):
             y_o, ix = m & 3, m >> 2
-            x_o = 2 * e + (ix ^ e ^ (q & 1))
+            x_o = 2 * (e ^ (q & 1)) + (ix ^ e)
             dx, dy = (x_o - x_at) & 3, (y_o - y_at) & 3
             for flip, ref in enumerate((keep, send)):
                 c_o = core ^ flip
@@ -293,19 +304,25 @@
     )
 
 
+def in_hbm(array):
+    return pltpu.with_memory_space_constraint(array, pltpu.HBM)
+
+
 def per_device(source, receiver, classes, coef_table, freq_list):
-    q = lax.axis_index("depth")
+    d = lax.axis_index("depth")
     f = lax.axis_index("freq")
     zh, x_at, y_at, core = f >> 5, (f >> 3) & 3, (f >> 1) & 3, f & 1
-    starts = [window_start((q + step) & 3) for step in (0, 2, 1, -1)]
-    levels = [(q + step) & 3 for step in (0, 2, -1, 1)]
+    z = 4 * zh + d
+    q = chunk_at(z)
+    starts = [window_start(chunk_at((z + step) & 7)) for step in (0, 2 - 4 * core, 1, -1)]
+    levels = [(d + step) & 3 for step in (0, 2, -1, 1)]
     place = jnp.stack([q, x_at, y_at, core] + starts + levels).astype(jnp.int32)
     own, two, up, down = call(
         cut_windows,
         [(WINDOW, jnp.int32)] * 4,
         [SCALARS, REMOTE],
         [pltpu.VMEM((NX, NY), jnp.int32), pltpu.VMEM((HALVES, NX, LANES), jnp.int32), pltpu.SemaphoreType.DMA((4,))],
-    )(place, classes)
+    )(place, in_hbm(classes))
     class_windows = [
         own,
         lax.ppermute(two, AXES, along_z(lambda c: 2 if c == 0 else -2)),
@@ -322,7 +339,7 @@
         [pltpu.VMEM((2, 2, WIN, NY), jnp.float32), pltpu.SemaphoreType.DMA((2,))],
         flops=10**7,
         moved=4 * 2**20,
-    )(place, source, receiver)
+    )(place, in_hbm(source), in_hbm(receiver))
     half_image = ((32, HALVES, 4 * H, LANES), jnp.float32)
     keep, send = call(
         all_levels,
@@ -342,7 +359,7 @@
         part = mine.shape[0] // 4
         got = [lax.ppermute(mine[t * part : (t + 1) * part], AXES, axis(t)) for t in (1, 2, 3)]
         mine = mine[:part] + got[0] + got[1] + got[2]
-    sent = [lax.dynamic_index_in_dim(mine, p ^ zh, 0, keepdims=False) for p in (0, 1)]
+    sent = [lax.dynamic_index_in_dim(mine, p ^ sent_first(q, zh), 0, keepdims=False) for p in (0, 1)]
     got = [lax.ppermute(sent[p], AXES, to_owner(p)) for p in (0, 1)]
     (image,) = call(last_sum, [((4, 1, H, NY), jnp.float32)], [LOCAL, LOCAL])(*got)
     return image

time: 61.5 us -> 55.2 us (0.90)
  starting transfers between devices: 26.2 us -> 22 us
  local copies, waits for them, and re-layouts: 3.54 us -> 0.51 us
  Pallas kernels: 12.5 us -> 13.7 us
    ppermute x2, starting transfers between devices: 8.04 us -> 4.96 us  [per_device(): got = [lax.ppermute(sent[p], AXES, to_owner(p)) for p in (0, 1)]]
    unnamed x8 -> x2, local copies, waits for them, and re-layouts: 3.03 us -> 0.01 us
    ppermute x2, waiting for transfers between devices: 6.49 us -> 4.69 us  [per_device(): got = [lax.ppermute(sent[p], AXES, to_owner(p)) for p in (0, 1)]]
    ppermute x6, waiting for transfers between devices: 8.64 us -> 10.1 us  [per_device(): lax.ppermute(mine[t * part:(t + 1) * part], AXES, axis(t))]
    ppermute x6, starting transfers between devices: 11.6 us -> 10.4 us  [per_device(): lax.ppermute(mine[t * part:(t + 1) * part], AXES, axis(t))]
    pallas_call x1, Pallas kernels: 2.73 us -> 3.37 us  [per_device(): call(first_terms, [(TERMS, jnp.float32)], [SCALARS, REMOTE, REMOTE], [plt...]
  transfers between devices with their start and end apart: 12 -> 12, of which waited for: 6 -> 10; matrix products, arithmetic and copies ran while one was open for 1% -> 1% of each run, Pallas kernels for 4% -> 6%
where the time goes in v3:
time: 55.2 us; the launch traced here: 55.1 us
  starting transfers between devices  22 us (40%)
  waiting for transfers between devices  17.8 us (32%)
  Pallas kernels  13.7 us (25%)
  between operations  0.77 us (1%)
    ppermute x6, starting transfers between devices, per_device(): lax.ppermute(mine[t * part:(t + 1) * part], AXES, axis(t))  10.4 us
    ppermute x6, waiting for transfers between devices, per_device(): lax.ppermute(mine[t * part:(t + 1) * part], AXES, axis(t))  10.1 us
    pallas_call x1, Pallas kernels, per_device(): call(all_levels, [half_image, half_image], [SCALARS] + [LOCAL] * 6, [pltp...  7.58 us
    ppermute x2, starting transfers between devices, per_device(): got = [lax.ppermute(sent[p], AXES, to_owner(p)) for p in (0, 1)]  4.96 us
    ppermute x2, waiting for transfers between devices, per_device(): got = [lax.ppermute(sent[p], AXES, to_owner(p)) for p in (0, 1)]  4.69 us
    pallas_call x1, Pallas kernels, per_device(): call(first_terms, [(TERMS, jnp.float32)], [SCALARS, REMOTE, REMOTE], [plt...  3.37 us
    ppermute x1, starting transfers between devices, per_device(): lax.ppermute(two, AXES, along_z(lambda c: 2 if c == 0 else -2))  3.35 us
    ppermute x1, starting transfers between devices, per_device(): lax.ppermute(up, AXES, along_z(lambda c: 1))  3.13 us
  transfers between devices with their start and end apart: 12, of which 10 were waited for; matrix products, arithmetic and copies ran while one was open for 1% of the time, Pallas kernels for 6%

profile of v3, /device:TPU:32, one launch (start us, length us, event | category | flops | bytes accessed | tf_op | source)
XLA Modules:
  0.0 55.1 jit_solution(8774623395518821197)
XLA Ops:
  0.0 0.0 copy-start
  0.0 0.1 stack.51.place
  0.1 2.0 %shard_map.56 = (s32[2,112,128]{2,1,0:T(8,128)S(1)}, s32[2,112,128]{2,1,0:T(8,128)S(1)}, s32[2,112,128]{2,1,0:T(8,128)S(1)}, s32[2,112,128]{2,1,0:T(8,128)S(1)}) custom-call(s32[12]{0:T(128)S(1)} %stack.51.place, s32[1,256,256]{2,1,0:T(8,128)} %classes.1), custom_call_target="tpu_custom_call" | custom-call | tf_op jit(solution)/shard_map/pallas_call | solution.py:320
  2.1 3.3 %collective-permute-start = (s32[2,112,128]{2,1,0:T(8,128)S(1)}, s32[2,112,128]{2,1,0:T(8,128)S(1)}, u32[]{:S(2)}, u32[]{:S(2)}) collective-permute-start(s32[2,112,128]{2,1,0:T(8,128)S(1)} %get-tuple-element.12), channel_id=1, source_target_pairs={{0,128},{1,161},{2,130},{3,163},{4,132},{5,165},{6,134},{7,167},{8... | collective-permute-start | bytes 344072 | tf_op jit(solution)/shard_map/ppermute | solution.py:328
  5.5 3.1 %collective-permute-start.1 = (s32[2,112,128]{2,1,0:T(8,128)S(1)}, s32[2,112,128]{2,1,0:T(8,128)S(1)}, u32[]{:S(2)}, u32[]{:S(2)}) collective-permute-start(s32[2,112,128]{2,1,0:T(8,128)S(1)} %get-tuple-element.13), channel_id=1, source_target_pairs={{0,64},{1,65},{2,66},{3,67},{4,68},{5,69},{6,70},{7,71},{8,72},{9,... | collective-permute-start | bytes 344072 | tf_op jit(solution)/shard_map/ppermute | solution.py:329
  8.6 0.0 collective-permute-start.2
  9.2 0.0 copy-done
  9.2 0.2 constant_dynamic-slice_fusion
  9.4 0.1 copy.6
  9.6 3.4 %shard_map.55.first = f32[6,4,2,128,128]{4,3,2,1,0:T(8,128)S(1)} custom-call(s32[12]{0:T(128)S(1)} %stack.51.place, f32[1,2,256,256]{3,2,1,0:T(8,128)} %src.1, f32[1,2,256,256]{3,2,1,0:T(8,128)} %rec.1), custom_call_target="tpu_custom_call" | custom-call | flops 10000000 | bytes 4194304 | tf_op jit(solution)/shard_map/pallas_call | solution.py:335
  13.0 0.0 collective-permute-done.w1
  13.0 0.0 collective-permute-done.1.w2
  13.0 0.4 collective-permute-done.2.w3
  13.4 7.6 %shard_map.57 = (f32[32,2,32,128]{3,2,1,0:T(8,128)S(1)}, f32[32,2,32,128]{3,2,1,0:T(8,128)S(1)}) custom-call(s32[12]{0:T(128)S(1)} %stack.51.place, f32[6,4,2,128,128]{4,3,2,1,0:T(8,128)S(1)} %shard_map.55.first, s32[2,112,128]{2,1,0:T(8,128)S(1)} %get-tuple-element.11.w0, s32[2,112,128]{2,1,0:T(8,128)S(1)} %collective-permute-done.w1, ...), custom_call_target="tpu_custom_call" | custom-call | flops 50000000 | bytes 4194304 | tf_op jit(solution)/shard_map/pallas_call | solution.py:344
  21.0 0.1 collective-permute-start.3
  21.1 2.6 %collective-permute-done.3 = f32[32,2,32,128]{3,2,1,0:T(8,128)S(1)} collective-permute-done((f32[32,2,32,128]{3,2,1,0:T(8,128)S(1)}, f32[32,2,32,128]{3,2,1,0:T(8,128)S(1)}, u32[]{:S(2)}, u32[]{:S(2)}) %collective-permute-start.3) | collective-permute-done | bytes 1048608 | tf_op jit(solution)/shard_map/ppermute | solution.py:357
  23.7 0.2 add.106
  23.9 0.1 fusion.4
  24.0 1.6 %collective-permute-start.4 = (f32[8,2,32,128]{3,2,1,0:T(8,128)S(1)}, f32[8,2,32,128]{3,2,1,0:T(8,128)S(1)}, u32[]{:S(2)}, u32[]{:S(2)}) collective-permute-start(f32[8,2,32,128]{3,2,1,0:T(8,128)S(1)} %get-tuple-element.17), channel_id=1, source_target_pairs={{0,8},{1,3},{2,10},{3,5},{4,12},{5,7},{6,14},{7,1},{8,16},{9,11},{... | collective-permute-start | bytes 786440 | tf_op jit(solution)/shard_map/ppermute | solution.py:360
  25.6 1.7 %collective-permute-start.6 = (f32[8,2,32,128]{3,2,1,0:T(8,128)S(1)}, f32[8,2,32,128]{3,2,1,0:T(8,128)S(1)}, u32[]{:S(2)}, u32[]{:S(2)}) collective-permute-start(f32[8,2,32,128]{3,2,1,0:T(8,128)S(1)} %get-tuple-element.18), channel_id=1, source_target_pairs={{0,24},{1,7},{2,26},{3,1},{4,28},{5,3},{6,30},{7,5},{8,0},{9,15},{... | collective-permute-start | bytes 786440 | tf_op jit(solution)/shard_map/ppermute | solution.py:360
  27.3 1.8 %collective-permute-start.5 = (f32[8,2,32,128]{3,2,1,0:T(8,128)S(1)}, f32[8,2,32,128]{3,2,1,0:T(8,128)S(1)}, u32[]{:S(2)}, u32[]{:S(2)}) collective-permute-start(f32[8,2,32,128]{3,2,1,0:T(8,128)S(1)} %get-tuple-element.19), channel_id=1, source_target_pairs={{0,16},{1,5},{2,18},{3,7},{4,20},{5,1},{6,22},{7,3},{8,24},{9,13},... | collective-permute-start | bytes 786440 | tf_op jit(solution)/shard_map/ppermute | solution.py:360
  29.1 2.5 %collective-permute-done.4 = f32[8,2,32,128]{3,2,1,0:T(8,128)S(1)} collective-permute-done((f32[8,2,32,128]{3,2,1,0:T(8,128)S(1)}, f32[8,2,32,128]{3,2,1,0:T(8,128)S(1)}, u32[]{:S(2)}, u32[]{:S(2)}) %collective-permute-start.4) | collective-permute-done | bytes 262176 | tf_op jit(solution)/shard_map/ppermute | solution.py:360
  31.7 2.4 %collective-permute-done.6 = f32[8,2,32,128]{3,2,1,0:T(8,128)S(1)} collective-permute-done((f32[8,2,32,128]{3,2,1,0:T(8,128)S(1)}, f32[8,2,32,128]{3,2,1,0:T(8,128)S(1)}, u32[]{:S(2)}, u32[]{:S(2)}) %collective-permute-start.6) | collective-permute-done | bytes 262176 | tf_op jit(solution)/shard_map/ppermute | solution.py:360
  34.0 1.4 %collective-permute-done.5 = f32[8,2,32,128]{3,2,1,0:T(8,128)S(1)} collective-permute-done((f32[8,2,32,128]{3,2,1,0:T(8,128)S(1)}, f32[8,2,32,128]{3,2,1,0:T(8,128)S(1)}, u32[]{:S(2)}, u32[]{:S(2)}) %collective-permute-start.5) | collective-permute-done | bytes 262176 | tf_op jit(solution)/shard_map/ppermute | solution.py:360
  35.5 0.1 fusion.1
  35.6 1.7 %collective-permute-start.7 = (f32[2,2,32,128]{3,2,1,0:T(8,128)S(1)}, f32[2,2,32,128]{3,2,1,0:T(8,128)S(1)}, u32[]{:S(2)}, u32[]{:S(2)}) collective-permute-start(f32[2,2,32,128]{3,2,1,0:T(8,128)S(1)} %get-tuple-element.20), channel_id=1, source_target_pairs={{0,2},{1,9},{2,4},{3,11},{4,6},{5,13},{6,0},{7,15},{8,10},{9,17},{... | collective-permute-start | bytes 196616 | tf_op jit(solution)/shard_map/ppermute | solution.py:360
  37.2 1.7 %collective-permute-start.9 = (f32[2,2,32,128]{3,2,1,0:T(8,128)S(1)}, f32[2,2,32,128]{3,2,1,0:T(8,128)S(1)}, u32[]{:S(2)}, u32[]{:S(2)}) collective-permute-start(f32[2,2,32,128]{3,2,1,0:T(8,128)S(1)} %get-tuple-element.21), channel_id=1, source_target_pairs={{0,6},{1,25},{2,0},{3,27},{4,2},{5,29},{6,4},{7,31},{8,14},{9,1},{... | collective-permute-start | bytes 196616 | tf_op jit(solution)/shard_map/ppermute | solution.py:360
  38.9 2.0 %collective-permute-start.8 = (f32[2,2,32,128]{3,2,1,0:T(8,128)S(1)}, f32[2,2,32,128]{3,2,1,0:T(8,128)S(1)}, u32[]{:S(2)}, u32[]{:S(2)}) collective-permute-start(f32[2,2,32,128]{3,2,1,0:T(8,128)S(1)} %get-tuple-element.22), channel_id=1, source_target_pairs={{0,4},{1,17},{2,6},{3,19},{4,0},{5,21},{6,2},{7,23},{8,12},{9,25},... | collective-permute-start | bytes 196616 | tf_op jit(solution)/shard_map/ppermute | solution.py:360
  40.9 0.3 collective-permute-done.7
  41.1 0.4 collective-permute-done.9
  41.5 3.2 %collective-permute-done.8 = f32[2,2,32,128]{3,2,1,0:T(8,128)S(1)} collective-permute-done((f32[2,2,32,128]{3,2,1,0:T(8,128)S(1)}, f32[2,2,32,128]{3,2,1,0:T(8,128)S(1)}, u32[]{:S(2)}, u32[]{:S(2)}) %collective-permute-start.8) | collective-permute-done | bytes 65568 | tf_op jit(solution)/shard_map/ppermute | solution.py:360
  44.7 1.3 %collective-permute-start.11 = (f32[2,32,128]{2,1,0:T(8,128)S(1)}, f32[2,32,128]{2,1,0:T(8,128)S(1)}, u32[]{:S(2)}, u32[]{:S(2)}) collective-permute-start(f32[2,32,128]{2,1,0:T(8,128)S(1)} %get-tuple-element.23), channel_id=1, source_target_pairs={{0,120},{1,121},{2,122},{3,123},{4,124},{5,125},{6,126},{7,127},{8... | collective-permute-start | bytes 98312 | tf_op jit(solution)/shard_map/ppermute | solution.py:363
  46.0 3.6 %collective-permute-start.10 = (f32[2,32,128]{2,1,0:T(8,128)S(1)}, f32[2,32,128]{2,1,0:T(8,128)S(1)}, u32[]{:S(2)}, u32[]{:S(2)}) collective-permute-start(f32[2,32,128]{2,1,0:T(8,128)S(1)} %get-tuple-element.24), channel_id=1, source_target_pairs={{0,184},{1,185},{2,186},{3,187},{4,188},{5,189},{6,190},{7,191},{8... | collective-permute-start | bytes 98312 | tf_op jit(solution)/shard_map/ppermute | solution.py:363
  49.7 0.2 collective-permute-done.11.b
  49.9 4.5 %collective-permute-done.10.a = f32[2,32,128]{2,1,0:T(8,128)S(1)} collective-permute-done((f32[2,32,128]{2,1,0:T(8,128)S(1)}, f32[2,32,128]{2,1,0:T(8,128)S(1)}, u32[]{:S(2)}, u32[]{:S(2)}) %collective-permute-start.10) | collective-permute-done | bytes 32800 | tf_op jit(solution)/shard_map/ppermute | solution.py:363
  54.4 0.7 %shard_map.58 = f32[4,1,8,256]{3,2,1,0:T(8,128)} custom-call(f32[2,32,128]{2,1,0:T(8,128)S(1)} %collective-permute-done.10.a, f32[2,32,128]{2,1,0:T(8,128)S(1)} %collective-permute-done.11.b), custom_call_target="tpu_custom_call" | custom-call | tf_op jit(solution)/shard_map/pallas_call | solution.py:364
  (6 shorter events, 0.1 us)
Async XLA Ops:
  0.0 9.2 %copy-start = (f32[16,64,2,6]{1,2,3,0:T(2,128)S(1)}, f32[16,64,2,6]{1,2,3,0:T(2,128)}, u32[]{:S(2)}) copy-start(f32[16,64,2,6]{1,2,3,0:T(2,128)} %param.8) | copy-start | bytes 147460
  2.1 10.9 %collective-permute-start = (s32[2,112,128]{2,1,0:T(8,128)S(1)}, s32[2,112,128]{2,1,0:T(8,128)S(1)}, u32[]{:S(2)}, u32[]{:S(2)}) collective-permute-start(s32[2,112,128]{2,1,0:T(8,128)S(1)} %get-tuple-element.12), channel_id=1, source_target_pairs={{0,128},{1,161},{2,130},{3,163},{4,132},{5,165},{6,134},{7,167},{8... | collective-permute-start | bytes 344072 | tf_op jit(solution)/shard_map/ppermute | solution.py:328
  5.5 7.5 %collective-permute-start.1 = (s32[2,112,128]{2,1,0:T(8,128)S(1)}, s32[2,112,128]{2,1,0:T(8,128)S(1)}, u32[]{:S(2)}, u32[]{:S(2)}) collective-permute-start(s32[2,112,128]{2,1,0:T(8,128)S(1)} %get-tuple-element.13), channel_id=1, source_target_pairs={{0,64},{1,65},{2,66},{3,67},{4,68},{5,69},{6,70},{7,71},{8,72},{9,... | collective-permute-start | bytes 344072 | tf_op jit(solution)/shard_map/ppermute | solution.py:329
  8.6 4.8 %collective-permute-start.2 = (s32[2,112,128]{2,1,0:T(8,128)S(1)}, s32[2,112,128]{2,1,0:T(8,128)S(1)}, u32[]{:S(2)}, u32[]{:S(2)}) collective-permute-start(s32[2,112,128]{2,1,0:T(8,128)S(1)} %get-tuple-element.14), channel_id=1, source_target_pairs={{0,224},{1,225},{2,226},{3,227},{4,228},{5,229},{6,230},{7,231},{8... | collective-permute-start | bytes 344072 | tf_op jit(solution)/shard_map/ppermute | solution.py:330
  21.0 2.7 %collective-permute-start.3 = (f32[32,2,32,128]{3,2,1,0:T(8,128)S(1)}, f32[32,2,32,128]{3,2,1,0:T(8,128)S(1)}, u32[]{:S(2)}, u32[]{:S(2)}) collective-permute-start(f32[32,2,32,128]{3,2,1,0:T(8,128)S(1)} %get-tuple-element.16), channel_id=1, source_target_pairs={{0,1},{1,0},{2,3},{3,2},{4,5},{5,4},{6,7},{7,6},{8,9},{9,8},{10,11... | collective-permute-start | bytes 3145736 | tf_op jit(solution)/shard_map/ppermute | solution.py:357
  24.0 7.7 %collective-permute-start.4 = (f32[8,2,32,128]{3,2,1,0:T(8,128)S(1)}, f32[8,2,32,128]{3,2,1,0:T(8,128)S(1)}, u32[]{:S(2)}, u32[]{:S(2)}) collective-permute-start(f32[8,2,32,128]{3,2,1,0:T(8,128)S(1)} %get-tuple-element.17), channel_id=1, source_target_pairs={{0,8},{1,3},{2,10},{3,5},{4,12},{5,7},{6,14},{7,1},{8,16},{9,11},{... | collective-permute-start | bytes 786440 | tf_op jit(solution)/shard_map/ppermute | solution.py:360
  25.6 8.5 %collective-permute-start.6 = (f32[8,2,32,128]{3,2,1,0:T(8,128)S(1)}, f32[8,2,32,128]{3,2,1,0:T(8,128)S(1)}, u32[]{:S(2)}, u32[]{:S(2)}) collective-permute-start(f32[8,2,32,128]{3,2,1,0:T(8,128)S(1)} %get-tuple-element.18), channel_id=1, source_target_pairs={{0,24},{1,7},{2,26},{3,1},{4,28},{5,3},{6,30},{7,5},{8,0},{9,15},{... | collective-permute-start | bytes 786440 | tf_op jit(solution)/shard_map/ppermute | solution.py:360
  27.3 8.1 %collective-permute-start.5 = (f32[8,2,32,128]{3,2,1,0:T(8,128)S(1)}, f32[8,2,32,128]{3,2,1,0:T(8,128)S(1)}, u32[]{:S(2)}, u32[]{:S(2)}) collective-permute-start(f32[8,2,32,128]{3,2,1,0:T(8,128)S(1)} %get-tuple-element.19), channel_id=1, source_target_pairs={{0,16},{1,5},{2,18},{3,7},{4,20},{5,1},{6,22},{7,3},{8,24},{9,13},... | collective-permute-start | bytes 786440 | tf_op jit(solution)/shard_map/ppermute | solution.py:360
  35.6 5.6 %collective-permute-start.7 = (f32[2,2,32,128]{3,2,1,0:T(8,128)S(1)}, f32[2,2,32,128]{3,2,1,0:T(8,128)S(1)}, u32[]{:S(2)}, u32[]{:S(2)}) collective-permute-start(f32[2,2,32,128]{3,2,1,0:T(8,128)S(1)} %get-tuple-element.20), channel_id=1, source_target_pairs={{0,2},{1,9},{2,4},{3,11},{4,6},{5,13},{6,0},{7,15},{8,10},{9,17},{... | collective-permute-start | bytes 196616 | tf_op jit(solution)/shard_map/ppermute | solution.py:360
  37.2 4.3 %collective-permute-start.9 = (f32[2,2,32,128]{3,2,1,0:T(8,128)S(1)}, f32[2,2,32,128]{3,2,1,0:T(8,128)S(1)}, u32[]{:S(2)}, u32[]{:S(2)}) collective-permute-start(f32[2,2,32,128]{3,2,1,0:T(8,128)S(1)} %get-tuple-element.21), channel_id=1, source_target_pairs={{0,6},{1,25},{2,0},{3,27},{4,2},{5,29},{6,4},{7,31},{8,14},{9,1},{... | collective-permute-start | bytes 196616 | tf_op jit(solution)/shard_map/ppermute | solution.py:360
  38.9 5.8 %collective-permute-start.8 = (f32[2,2,32,128]{3,2,1,0:T(8,128)S(1)}, f32[2,2,32,128]{3,2,1,0:T(8,128)S(1)}, u32[]{:S(2)}, u32[]{:S(2)}) collective-permute-start(f32[2,2,32,128]{3,2,1,0:T(8,128)S(1)} %get-tuple-element.22), channel_id=1, source_target_pairs={{0,4},{1,17},{2,6},{3,19},{4,0},{5,21},{6,2},{7,23},{8,12},{9,25},... | collective-permute-start | bytes 196616 | tf_op jit(solution)/shard_map/ppermute | solution.py:360
  44.7 5.2 %collective-permute-start.11 = (f32[2,32,128]{2,1,0:T(8,128)S(1)}, f32[2,32,128]{2,1,0:T(8,128)S(1)}, u32[]{:S(2)}, u32[]{:S(2)}) collective-permute-start(f32[2,32,128]{2,1,0:T(8,128)S(1)} %get-tuple-element.23), channel_id=1, source_target_pairs={{0,120},{1,121},{2,122},{3,123},{4,124},{5,125},{6,126},{7,127},{8... | collective-permute-start | bytes 98312 | tf_op jit(solution)/shard_map/ppermute | solution.py:363
  46.0 8.3 %collective-permute-start.10 = (f32[2,32,128]{2,1,0:T(8,128)S(1)}, f32[2,32,128]{2,1,0:T(8,128)S(1)}, u32[]{:S(2)}, u32[]{:S(2)}) collective-permute-start(f32[2,32,128]{2,1,0:T(8,128)S(1)} %get-tuple-element.24), channel_id=1, source_target_pairs={{0,184},{1,185},{2,186},{3,187},{4,188},{5,189},{6,190},{7,191},{8... | collective-permute-start | bytes 98312 | tf_op jit(solution)/shard_map/ppermute | solution.py:363

commit v4 on v3

--- a/solution.py
+++ b/solution.py
@@ -18,9 +18,7 @@
 STEPS = WIN // 8
 PAD = 8
 ROWS = WIN + 2 * PAD
-COMBINE = 7
 IMAGE = 4
-SKEW = 3
 COMPS = 2
 LIMIT = 32
 LANES = 128
@@ -110,7 +108,8 @@
     )
 
 
-def cut_windows(place, classes, own, two, up, down, raw, parted, sem):
+def cut_windows(place, classes, src, rec, own, two, up, down, fields, raw, parted, sem, field_sem):
+    here = pl.multiple_of(place[4], 8)
     quarter = NX // 4
     loads = []
     for n in range(4):
@@ -118,6 +117,11 @@
         cp = pltpu.make_async_copy(classes.at[0, rows, :], raw.at[rows, :], sem.at[n])
         cp.start()
         loads.append(cp)
+    field_loads = []
+    for n, ref in enumerate((src, rec)):
+        cp = pltpu.make_async_copy(ref.at[0, :, pl.ds(here, WIN), :], fields.at[n], field_sem.at[n])
+        cp.start()
+        field_loads.append(cp)
     for n in range(4):
         loads[n].wait()
         for r in range(quarter * n, quarter * (n + 1), 8):
@@ -128,21 +132,20 @@
         for half in range(HALVES):
             for tile in range(STEPS):
                 ref[half, 8 * tile : 8 * tile + 8, :] = parted[half, pl.ds(start + 8 * tile, 8), :]
-
-
-def stencil(field, comp):
+    for cp in field_loads:
+        cp.wait()
+
+
+def stencil(field, comp, tiles, top):
     lane = lanes_of()
     first_lane, last_lane = lane == 0, lane == LANES - 1
-    for step in range(STEPS + SKEW * (K - 2)):
-        for k in range(1, K):
-            tile = step - SKEW * (k - 1)
-            if not 0 <= tile < STEPS:
-                continue
-            r = PAD + 8 * tile
+    for k in range(1, K):
+        for tile in range(tiles):
+            at = pl.multiple_of(PAD + top, 8) + 8 * tile if not isinstance(top, int) else PAD + top + 8 * tile
             g, rest = [], []
             for half in range(HALVES):
-                v = field[k - 1, comp, half, r : r + 8, :]
-                h = 0.5 * (field[k - 1, comp, half, r - 1 : r + 7, :] + field[k - 1, comp, half, r + 1 : r + 9, :])
+                v = field[k - 1, comp, half, pl.ds(at, 8), :]
+                h = 0.5 * (field[k - 1, comp, half, pl.ds(at - 1, 8), :] + field[k - 1, comp, half, pl.ds(at + 1, 8), :])
                 g.append(h + v)
                 rest.append(h - v)
             before = jnp.where(first_lane, 0.0, pltpu.roll(g[1], 1, 1))
@@ -153,14 +156,14 @@
                 if k == 1:
                     w = 0.5 * w
                 else:
-                    w = w - field[k - 2, comp, half, r : r + 8, :]
-                field[k, comp, half, r : r + 8, :] = w
-
-
-def stencils(field):
+                    w = w - field[k - 2, comp, half, pl.ds(at, 8), :]
+                field[k, comp, half, pl.ds(at, 8), :] = w
+
+
+def stencils(field, tiles=STEPS, top=0):
     def some(step, carry):
         for part in range(COMPS):
-            stencil(field, COMPS * step + part)
+            stencil(field, COMPS * step + part, tiles, top)
         return carry
 
     lax.fori_loop(0, 4 // COMPS, some, 0)
@@ -175,20 +178,13 @@
                 field[k, comp, half, PAD + WIN : ROWS, :] = zero
 
 
-def first_terms(place, src, rec, field, raw, sem):
-    start = pl.multiple_of(place[4], 8)
-    loads = []
-    for n, ref in enumerate((src, rec)):
-        cp = pltpu.make_async_copy(ref.at[0, :, pl.ds(start, WIN), :], raw.at[n], sem.at[n])
-        cp.start()
-        loads.append(cp)
+def first_terms(fields, field):
     clear_ends(field)
     for n in range(2):
-        loads[n].wait()
         for part in range(2):
             for tile in range(STEPS):
                 r = 8 * tile
-                lo, hi = raw[n, part, r : r + 8, 0:LANES], raw[n, part, r : r + 8, LANES:NY]
+                lo, hi = fields[n, part, r : r + 8, 0:LANES], fields[n, part, r : r + 8, LANES:NY]
                 for half, v in enumerate(by_parity(lo, hi)):
                     field[0, 2 * n + part, half, PAD + r : PAD + r + 8, :] = v
     stencils(field)
@@ -207,11 +203,11 @@
     mirror = 7 - lax.broadcasted_iota(jnp.int32, (8, LANES), 0)
     base = pl.multiple_of(PAD + CHUNK * q - place[4], 8)
 
-    def finish(level, terms):
+    def finish(level, terms, tiles, top):
         def combine(step, carry):
             places = []
-            for part in range(COMBINE):
-                r = pl.multiple_of(PAD + 8 * (COMBINE * step + part), 8)
+            for part in range(tiles // 2):
+                r = pl.multiple_of(PAD + top + 8 * (tiles // 2 * step + part), 8)
                 places += [(half, r) for half in range(HALVES)]
 
             def look_up(half, r):
@@ -238,7 +234,7 @@
                 field[0, 3, half, pl.ds(r, 8), :] = p[3] + s[2]
             return carry
 
-        lax.fori_loop(0, STEPS // COMBINE, combine, 0)
+        lax.fori_loop(0, 2, combine, 0)
         lb = level >> 1
         e = (level ^ lb) & 1
 
@@ -265,14 +261,17 @@
 
         lax.fori_loop(0, 8 // IMAGE, image, 0)
 
-    finish(0, first)
-
-    def level_body(level, carry):
-        stencils(field)
-        finish(level, field)
-        return carry
-
-    lax.fori_loop(1, Z, level_body, 0)
+    def reach(rows):
+        tiles = (CHUNK + 2 * rows) // 8
+        return tiles, jnp.clip(CHUNK * q - place[4] - rows, 0, WIN - 8 * tiles)
+
+    finish(0, first, STEPS, 0)
+    stencils(field)
+    finish(1, field, *reach(16))
+    stencils(field, *reach(16))
+    finish(2, field, *reach(16))
+    stencils(field, *reach(8))
+    finish(3, field, *reach(8))
 
 
 def last_sum(a, b, out):
@@ -317,12 +316,17 @@
     starts = [window_start(chunk_at((z + step) & 7)) for step in (0, 2 - 4 * core, 1, -1)]
     levels = [(d + step) & 3 for step in (0, 2, -1, 1)]
     place = jnp.stack([q, x_at, y_at, core] + starts + levels).astype(jnp.int32)
-    own, two, up, down = call(
+    own, two, up, down, fields = call(
         cut_windows,
-        [(WINDOW, jnp.int32)] * 4,
-        [SCALARS, REMOTE],
-        [pltpu.VMEM((NX, NY), jnp.int32), pltpu.VMEM((HALVES, NX, LANES), jnp.int32), pltpu.SemaphoreType.DMA((4,))],
-    )(place, in_hbm(classes))
+        [(WINDOW, jnp.int32)] * 4 + [((2, 2, WIN, NY), jnp.float32)],
+        [SCALARS] + [REMOTE] * 3,
+        [
+            pltpu.VMEM((NX, NY), jnp.int32),
+            pltpu.VMEM((HALVES, NX, LANES), jnp.int32),
+            pltpu.SemaphoreType.DMA((4,)),
+            pltpu.SemaphoreType.DMA((2,)),
+        ],
+    )(place, in_hbm(classes), in_hbm(source), in_hbm(receiver))
     class_windows = [
         own,
         lax.ppermute(two, AXES, along_z(lambda c: 2 if c == 0 else -2)),
@@ -335,11 +339,10 @@
     (first,) = call(
         first_terms,
         [(TERMS, jnp.float32)],
-        [SCALARS, REMOTE, REMOTE],
-        [pltpu.VMEM((2, 2, WIN, NY), jnp.float32), pltpu.SemaphoreType.DMA((2,))],
+        [LOCAL],
         flops=10**7,
         moved=4 * 2**20,
-    )(place, in_hbm(source), in_hbm(receiver))
+    )(fields)
     half_image = ((32, HALVES, 4 * H, LANES), jnp.float32)
     keep, send = call(
         all_levels,

time: 55.2 us -> 54.7 us (level)
  Pallas kernels: 13.7 us -> 11.9 us
  waiting for transfers between devices: 17.8 us -> 19.2 us
    pallas_call x2, Pallas kernels: 5.38 us -> 3.94 us  [the longest x1 2.03 us: per_device(): call(cut_windows, [(WINDOW, jnp.int32)] * 4 + [((2, 2, WIN, NY), jnp.floa...]
    ppermute x1, waiting for transfers between devices: 0.01 us -> 0.72 us  [per_device(): lax.ppermute(up, AXES, along_z(lambda c: 1))]
  transfers between devices with their start and end apart: 12 -> 12, of which waited for: 10 -> 12; matrix products, arithmetic and copies ran while one was open for 1% -> 1% of each run, Pallas kernels for 6% -> 3%
where the time goes in v4:
time: 54.7 us; the launch traced here: 54.6 us
  starting transfers between devices  22 us (40%)
  waiting for transfers between devices  19.2 us (35%)
  Pallas kernels  11.9 us (22%)
  between operations  0.76 us (1%)
    ppermute x6, starting transfers between devices, per_device(): lax.ppermute(mine[t * part:(t + 1) * part], AXES, axis(t))  10.4 us
    ppermute x6, waiting for transfers between devices, per_device(): lax.ppermute(mine[t * part:(t + 1) * part], AXES, axis(t))  10.1 us
    pallas_call x1, Pallas kernels, per_device(): call(all_levels, [half_image, half_image], [SCALARS] + [LOCAL] * 6, [pltp...  7.23 us
    ppermute x2, starting transfers between devices, per_device(): got = [lax.ppermute(sent[p], AXES, to_owner(p)) for p in (0, 1)]  4.96 us
    ppermute x2, waiting for transfers between devices, per_device(): got = [lax.ppermute(sent[p], AXES, to_owner(p)) for p in (0, 1)]  4.53 us
    ppermute x1, starting transfers between devices, per_device(): lax.ppermute(two, AXES, along_z(lambda c: 2 if c == 0 else -2))  3.35 us
    ppermute x1, starting transfers between devices, per_device(): lax.ppermute(up, AXES, along_z(lambda c: 1))  3.13 us
    ppermute x1, waiting for transfers between devices, per_device(): mine = keep + lax.ppermute(send, AXES, CORE_SWAP)  2.65 us
  transfers between devices with their start and end apart: 12, of which 12 were waited for; matrix products, arithmetic and copies ran while one was open for 1% of the time, Pallas kernels for 3%

profile of v4, /device:TPU:32, one launch (start us, length us, event | category | flops | bytes accessed | tf_op | source)
XLA Modules:
  0.0 54.6 jit_solution(5781669121097511246)
XLA Ops:
  0.0 0.0 copy-start
  0.0 0.1 stack.51.place
  0.1 2.0 %shard_map.55 = (s32[2,112,128]{2,1,0:T(8,128)S(1)}, s32[2,112,128]{2,1,0:T(8,128)S(1)}, s32[2,112,128]{2,1,0:T(8,128)S(1)}, s32[2,112,128]{2,1,0:T(8,128)S(1)}, f32[2,2,112,256]{3,2,1,0:T(8,128)S(1)}) custom-call(s32[12]{0:T(128)S(1)} %stack.51.place, s32[1,256,256]{2,1,0:T(8,128)} %classes.1, f32[1,2,256,256]{3,2,1,0:T(8,128)} %src.1, f32[1,2,256,256]{3,2,1,0:T(8,128)} %rec.1), custom_call_target="tpu_custom_call" | custom-call | tf_op jit(solution)/shard_map/pallas_call | solution.py:319
  2.1 3.3 %collective-permute-start = (s32[2,112,128]{2,1,0:T(8,128)S(1)}, s32[2,112,128]{2,1,0:T(8,128)S(1)}, u32[]{:S(2)}, u32[]{:S(2)}) collective-permute-start(s32[2,112,128]{2,1,0:T(8,128)S(1)} %get-tuple-element.14), channel_id=1, source_target_pairs={{0,128},{1,161},{2,130},{3,163},{4,132},{5,165},{6,134},{7,167},{8... | collective-permute-start | bytes 344072 | tf_op jit(solution)/shard_map/ppermute | solution.py:332
  5.5 3.1 %collective-permute-start.1 = (s32[2,112,128]{2,1,0:T(8,128)S(1)}, s32[2,112,128]{2,1,0:T(8,128)S(1)}, u32[]{:S(2)}, u32[]{:S(2)}) collective-permute-start(s32[2,112,128]{2,1,0:T(8,128)S(1)} %get-tuple-element.15), channel_id=1, source_target_pairs={{0,64},{1,65},{2,66},{3,67},{4,68},{5,69},{6,70},{7,71},{8,72},{9,... | collective-permute-start | bytes 344072 | tf_op jit(solution)/shard_map/ppermute | solution.py:333
  8.6 0.0 collective-permute-start.2
  9.3 0.0 copy-done
  9.3 0.2 constant_dynamic-slice_fusion
  9.4 0.1 copy.6
  9.6 1.9 %shard_map.56.first = f32[6,4,2,128,128]{4,3,2,1,0:T(8,128)S(1)} custom-call(f32[2,2,112,256]{3,2,1,0:T(8,128)S(1)} %get-tuple-element.12.fields), custom_call_target="tpu_custom_call" | custom-call | flops 10000000 | bytes 4194304 | tf_op jit(solution)/shard_map/pallas_call | solution.py:339
  11.5 0.3 collective-permute-done.w1
  11.8 0.7 %collective-permute-done.1.w2 = s32[2,112,128]{2,1,0:T(8,128)S(1)} collective-permute-done((s32[2,112,128]{2,1,0:T(8,128)S(1)}, s32[2,112,128]{2,1,0:T(8,128)S(1)}, u32[]{:S(2)}, u32[]{:S(2)}) %collective-permute-start.1) | collective-permute-done | bytes 114720 | tf_op jit(solution)/shard_map/ppermute | solution.py:333
  12.5 0.9 %collective-permute-done.2.w3 = s32[2,112,128]{2,1,0:T(8,128)S(1)} collective-permute-done((s32[2,112,128]{2,1,0:T(8,128)S(1)}, s32[2,112,128]{2,1,0:T(8,128)S(1)}, u32[]{:S(2)}, u32[]{:S(2)}) %collective-permute-start.2) | collective-permute-done | bytes 114720 | tf_op jit(solution)/shard_map/ppermute | solution.py:334
  13.4 7.2 %shard_map.57 = (f32[32,2,32,128]{3,2,1,0:T(8,128)S(1)}, f32[32,2,32,128]{3,2,1,0:T(8,128)S(1)}) custom-call(s32[12]{0:T(128)S(1)} %stack.51.place, f32[6,4,2,128,128]{4,3,2,1,0:T(8,128)S(1)} %shard_map.56.first, s32[2,112,128]{2,1,0:T(8,128)S(1)} %get-tuple-element.13.w0, s32[2,112,128]{2,1,0:T(8,128)S(1)} %collective-permute-done.w1, ...), custom_call_target="tpu_custom_call" | custom-call | flops 50000000 | bytes 4194304 | tf_op jit(solution)/shard_map/pallas_call | solution.py:347
  20.6 0.1 collective-permute-start.3
  20.7 2.6 %collective-permute-done.3 = f32[32,2,32,128]{3,2,1,0:T(8,128)S(1)} collective-permute-done((f32[32,2,32,128]{3,2,1,0:T(8,128)S(1)}, f32[32,2,32,128]{3,2,1,0:T(8,128)S(1)}, u32[]{:S(2)}, u32[]{:S(2)}) %collective-permute-start.3) | collective-permute-done | bytes 1048608 | tf_op jit(solution)/shard_map/ppermute | solution.py:360
  23.4 0.2 add.106
  23.6 0.1 fusion.4
  23.7 1.6 %collective-permute-start.4 = (f32[8,2,32,128]{3,2,1,0:T(8,128)S(1)}, f32[8,2,32,128]{3,2,1,0:T(8,128)S(1)}, u32[]{:S(2)}, u32[]{:S(2)}) collective-permute-start(f32[8,2,32,128]{3,2,1,0:T(8,128)S(1)} %get-tuple-element.19), channel_id=1, source_target_pairs={{0,8},{1,3},{2,10},{3,5},{4,12},{5,7},{6,14},{7,1},{8,16},{9,11},{... | collective-permute-start | bytes 786440 | tf_op jit(solution)/shard_map/ppermute | solution.py:363
  25.2 1.7 %collective-permute-start.6 = (f32[8,2,32,128]{3,2,1,0:T(8,128)S(1)}, f32[8,2,32,128]{3,2,1,0:T(8,128)S(1)}, u32[]{:S(2)}, u32[]{:S(2)}) collective-permute-start(f32[8,2,32,128]{3,2,1,0:T(8,128)S(1)} %get-tuple-element.20), channel_id=1, source_target_pairs={{0,24},{1,7},{2,26},{3,1},{4,28},{5,3},{6,30},{7,5},{8,0},{9,15},{... | collective-permute-start | bytes 786440 | tf_op jit(solution)/shard_map/ppermute | solution.py:363
  27.0 1.8 %collective-permute-start.5 = (f32[8,2,32,128]{3,2,1,0:T(8,128)S(1)}, f32[8,2,32,128]{3,2,1,0:T(8,128)S(1)}, u32[]{:S(2)}, u32[]{:S(2)}) collective-permute-start(f32[8,2,32,128]{3,2,1,0:T(8,128)S(1)} %get-tuple-element.21), channel_id=1, source_target_pairs={{0,16},{1,5},{2,18},{3,7},{4,20},{5,1},{6,22},{7,3},{8,24},{9,13},... | collective-permute-start | bytes 786440 | tf_op jit(solution)/shard_map/ppermute | solution.py:363
  28.8 2.5 %collective-permute-done.4 = f32[8,2,32,128]{3,2,1,0:T(8,128)S(1)} collective-permute-done((f32[8,2,32,128]{3,2,1,0:T(8,128)S(1)}, f32[8,2,32,128]{3,2,1,0:T(8,128)S(1)}, u32[]{:S(2)}, u32[]{:S(2)}) %collective-permute-start.4) | collective-permute-done | bytes 262176 | tf_op jit(solution)/shard_map/ppermute | solution.py:363
  31.3 2.4 %collective-permute-done.6 = f32[8,2,32,128]{3,2,1,0:T(8,128)S(1)} collective-permute-done((f32[8,2,32,128]{3,2,1,0:T(8,128)S(1)}, f32[8,2,32,128]{3,2,1,0:T(8,128)S(1)}, u32[]{:S(2)}, u32[]{:S(2)}) %collective-permute-start.6) | collective-permute-done | bytes 262176 | tf_op jit(solution)/shard_map/ppermute | solution.py:363
  33.7 1.4 %collective-permute-done.5 = f32[8,2,32,128]{3,2,1,0:T(8,128)S(1)} collective-permute-done((f32[8,2,32,128]{3,2,1,0:T(8,128)S(1)}, f32[8,2,32,128]{3,2,1,0:T(8,128)S(1)}, u32[]{:S(2)}, u32[]{:S(2)}) %collective-permute-start.5) | collective-permute-done | bytes 262176 | tf_op jit(solution)/shard_map/ppermute | solution.py:363
  35.1 0.1 fusion.1
  35.2 1.7 %collective-permute-start.7 = (f32[2,2,32,128]{3,2,1,0:T(8,128)S(1)}, f32[2,2,32,128]{3,2,1,0:T(8,128)S(1)}, u32[]{:S(2)}, u32[]{:S(2)}) collective-permute-start(f32[2,2,32,128]{3,2,1,0:T(8,128)S(1)} %get-tuple-element.22), channel_id=1, source_target_pairs={{0,2},{1,9},{2,4},{3,11},{4,6},{5,13},{6,0},{7,15},{8,10},{9,17},{... | collective-permute-start | bytes 196616 | tf_op jit(solution)/shard_map/ppermute | solution.py:363
  36.9 1.7 %collective-permute-start.9 = (f32[2,2,32,128]{3,2,1,0:T(8,128)S(1)}, f32[2,2,32,128]{3,2,1,0:T(8,128)S(1)}, u32[]{:S(2)}, u32[]{:S(2)}) collective-permute-start(f32[2,2,32,128]{3,2,1,0:T(8,128)S(1)} %get-tuple-element.23), channel_id=1, source_target_pairs={{0,6},{1,25},{2,0},{3,27},{4,2},{5,29},{6,4},{7,31},{8,14},{9,1},{... | collective-permute-start | bytes 196616 | tf_op jit(solution)/shard_map/ppermute | solution.py:363
  38.6 2.0 %collective-permute-start.8 = (f32[2,2,32,128]{3,2,1,0:T(8,128)S(1)}, f32[2,2,32,128]{3,2,1,0:T(8,128)S(1)}, u32[]{:S(2)}, u32[]{:S(2)}) collective-permute-start(f32[2,2,32,128]{3,2,1,0:T(8,128)S(1)} %get-tuple-element.24), channel_id=1, source_target_pairs={{0,4},{1,17},{2,6},{3,19},{4,0},{5,21},{6,2},{7,23},{8,12},{9,25},... | collective-permute-start | bytes 196616 | tf_op jit(solution)/shard_map/ppermute | solution.py:363
  40.5 0.3 collective-permute-done.7
  40.8 0.4 collective-permute-done.9
  41.2 3.2 %collective-permute-done.8 = f32[2,2,32,128]{3,2,1,0:T(8,128)S(1)} collective-permute-done((f32[2,2,32,128]{3,2,1,0:T(8,128)S(1)}, f32[2,2,32,128]{3,2,1,0:T(8,128)S(1)}, u32[]{:S(2)}, u32[]{:S(2)}) %collective-permute-start.8) | collective-permute-done | bytes 65568 | tf_op jit(solution)/shard_map/ppermute | solution.py:363
  44.4 1.4 %collective-permute-start.11 = (f32[2,32,128]{2,1,0:T(8,128)S(1)}, f32[2,32,128]{2,1,0:T(8,128)S(1)}, u32[]{:S(2)}, u32[]{:S(2)}) collective-permute-start(f32[2,32,128]{2,1,0:T(8,128)S(1)} %get-tuple-element.25), channel_id=1, source_target_pairs={{0,120},{1,121},{2,122},{3,123},{4,124},{5,125},{6,126},{7,127},{8... | collective-permute-start | bytes 98312 | tf_op jit(solution)/shard_map/ppermute | solution.py:366
  45.7 3.6 %collective-permute-start.10 = (f32[2,32,128]{2,1,0:T(8,128)S(1)}, f32[2,32,128]{2,1,0:T(8,128)S(1)}, u32[]{:S(2)}, u32[]{:S(2)}) collective-permute-start(f32[2,32,128]{2,1,0:T(8,128)S(1)} %get-tuple-element.26), channel_id=1, source_target_pairs={{0,184},{1,185},{2,186},{3,187},{4,188},{5,189},{6,190},{7,191},{8... | collective-permute-start | bytes 98312 | tf_op jit(solution)/shard_map/ppermute | solution.py:366
  49.3 0.2 collective-permute-done.11.b
  49.6 4.3 %collective-permute-done.10.a = f32[2,32,128]{2,1,0:T(8,128)S(1)} collective-permute-done((f32[2,32,128]{2,1,0:T(8,128)S(1)}, f32[2,32,128]{2,1,0:T(8,128)S(1)}, u32[]{:S(2)}, u32[]{:S(2)}) %collective-permute-start.10) | collective-permute-done | bytes 32800 | tf_op jit(solution)/shard_map/ppermute | solution.py:366
  53.9 0.7 %shard_map.58 = f32[4,1,8,256]{3,2,1,0:T(8,128)} custom-call(f32[2,32,128]{2,1,0:T(8,128)S(1)} %collective-permute-done.10.a, f32[2,32,128]{2,1,0:T(8,128)S(1)} %collective-permute-done.11.b), custom_call_target="tpu_custom_call" | custom-call | tf_op jit(solution)/shard_map/pallas_call | solution.py:367
  (6 shorter events, 0.1 us)
Async XLA Ops:
  0.0 9.3 %copy-start = (f32[16,64,2,6]{1,2,3,0:T(2,128)S(1)}, f32[16,64,2,6]{1,2,3,0:T(2,128)}, u32[]{:S(2)}) copy-start(f32[16,64,2,6]{1,2,3,0:T(2,128)} %param.8) | copy-start | bytes 147460
  2.1 9.7 %collective-permute-start = (s32[2,112,128]{2,1,0:T(8,128)S(1)}, s32[2,112,128]{2,1,0:T(8,128)S(1)}, u32[]{:S(2)}, u32[]{:S(2)}) collective-permute-start(s32[2,112,128]{2,1,0:T(8,128)S(1)} %get-tuple-element.14), channel_id=1, source_target_pairs={{0,128},{1,161},{2,130},{3,163},{4,132},{5,165},{6,134},{7,167},{8... | collective-permute-start | bytes 344072 | tf_op jit(solution)/shard_map/ppermute | solution.py:332
  5.5 7.0 %collective-permute-start.1 = (s32[2,112,128]{2,1,0:T(8,128)S(1)}, s32[2,112,128]{2,1,0:T(8,128)S(1)}, u32[]{:S(2)}, u32[]{:S(2)}) collective-permute-start(s32[2,112,128]{2,1,0:T(8,128)S(1)} %get-tuple-element.15), channel_id=1, source_target_pairs={{0,64},{1,65},{2,66},{3,67},{4,68},{5,69},{6,70},{7,71},{8,72},{9,... | collective-permute-start | bytes 344072 | tf_op jit(solution)/shard_map/ppermute | solution.py:333
  8.6 4.8 %collective-permute-start.2 = (s32[2,112,128]{2,1,0:T(8,128)S(1)}, s32[2,112,128]{2,1,0:T(8,128)S(1)}, u32[]{:S(2)}, u32[]{:S(2)}) collective-permute-start(s32[2,112,128]{2,1,0:T(8,128)S(1)} %get-tuple-element.16), channel_id=1, source_target_pairs={{0,224},{1,225},{2,226},{3,227},{4,228},{5,229},{6,230},{7,231},{8... | collective-permute-start | bytes 344072 | tf_op jit(solution)/shard_map/ppermute | solution.py:334
  20.6 2.7 %collective-permute-start.3 = (f32[32,2,32,128]{3,2,1,0:T(8,128)S(1)}, f32[32,2,32,128]{3,2,1,0:T(8,128)S(1)}, u32[]{:S(2)}, u32[]{:S(2)}) collective-permute-start(f32[32,2,32,128]{3,2,1,0:T(8,128)S(1)} %get-tuple-element.18), channel_id=1, source_target_pairs={{0,1},{1,0},{2,3},{3,2},{4,5},{5,4},{6,7},{7,6},{8,9},{9,8},{10,11... | collective-permute-start | bytes 3145736 | tf_op jit(solution)/shard_map/ppermute | solution.py:360
  23.7 7.7 %collective-permute-start.4 = (f32[8,2,32,128]{3,2,1,0:T(8,128)S(1)}, f32[8,2,32,128]{3,2,1,0:T(8,128)S(1)}, u32[]{:S(2)}, u32[]{:S(2)}) collective-permute-start(f32[8,2,32,128]{3,2,1,0:T(8,128)S(1)} %get-tuple-element.19), channel_id=1, source_target_pairs={{0,8},{1,3},{2,10},{3,5},{4,12},{5,7},{6,14},{7,1},{8,16},{9,11},{... | collective-permute-start | bytes 786440 | tf_op jit(solution)/shard_map/ppermute | solution.py:363
  25.2 8.5 %collective-permute-start.6 = (f32[8,2,32,128]{3,2,1,0:T(8,128)S(1)}, f32[8,2,32,128]{3,2,1,0:T(8,128)S(1)}, u32[]{:S(2)}, u32[]{:S(2)}) collective-permute-start(f32[8,2,32,128]{3,2,1,0:T(8,128)S(1)} %get-tuple-element.20), channel_id=1, source_target_pairs={{0,24},{1,7},{2,26},{3,1},{4,28},{5,3},{6,30},{7,5},{8,0},{9,15},{... | collective-permute-start | bytes 786440 | tf_op jit(solution)/shard_map/ppermute | solution.py:363
  27.0 8.1 %collective-permute-start.5 = (f32[8,2,32,128]{3,2,1,0:T(8,128)S(1)}, f32[8,2,32,128]{3,2,1,0:T(8,128)S(1)}, u32[]{:S(2)}, u32[]{:S(2)}) collective-permute-start(f32[8,2,32,128]{3,2,1,0:T(8,128)S(1)} %get-tuple-element.21), channel_id=1, source_target_pairs={{0,16},{1,5},{2,18},{3,7},{4,20},{5,1},{6,22},{7,3},{8,24},{9,13},... | collective-permute-start | bytes 786440 | tf_op jit(solution)/shard_map/ppermute | solution.py:363
  35.2 5.6 %collective-permute-start.7 = (f32[2,2,32,128]{3,2,1,0:T(8,128)S(1)}, f32[2,2,32,128]{3,2,1,0:T(8,128)S(1)}, u32[]{:S(2)}, u32[]{:S(2)}) collective-permute-start(f32[2,2,32,128]{3,2,1,0:T(8,128)S(1)} %get-tuple-element.22), channel_id=1, source_target_pairs={{0,2},{1,9},{2,4},{3,11},{4,6},{5,13},{6,0},{7,15},{8,10},{9,17},{... | collective-permute-start | bytes 196616 | tf_op jit(solution)/shard_map/ppermute | solution.py:363
  36.9 4.3 %collective-permute-start.9 = (f32[2,2,32,128]{3,2,1,0:T(8,128)S(1)}, f32[2,2,32,128]{3,2,1,0:T(8,128)S(1)}, u32[]{:S(2)}, u32[]{:S(2)}) collective-permute-start(f32[2,2,32,128]{3,2,1,0:T(8,128)S(1)} %get-tuple-element.23), channel_id=1, source_target_pairs={{0,6},{1,25},{2,0},{3,27},{4,2},{5,29},{6,4},{7,31},{8,14},{9,1},{... | collective-permute-start | bytes 196616 | tf_op jit(solution)/shard_map/ppermute | solution.py:363
  38.6 5.8 %collective-permute-start.8 = (f32[2,2,32,128]{3,2,1,0:T(8,128)S(1)}, f32[2,2,32,128]{3,2,1,0:T(8,128)S(1)}, u32[]{:S(2)}, u32[]{:S(2)}) collective-permute-start(f32[2,2,32,128]{3,2,1,0:T(8,128)S(1)} %get-tuple-element.24), channel_id=1, source_target_pairs={{0,4},{1,17},{2,6},{3,19},{4,0},{5,21},{6,2},{7,23},{8,12},{9,25},... | collective-permute-start | bytes 196616 | tf_op jit(solution)/shard_map/ppermute | solution.py:363
  44.4 5.2 %collective-permute-start.11 = (f32[2,32,128]{2,1,0:T(8,128)S(1)}, f32[2,32,128]{2,1,0:T(8,128)S(1)}, u32[]{:S(2)}, u32[]{:S(2)}) collective-permute-start(f32[2,32,128]{2,1,0:T(8,128)S(1)} %get-tuple-element.25), channel_id=1, source_target_pairs={{0,120},{1,121},{2,122},{3,123},{4,124},{5,125},{6,126},{7,127},{8... | collective-permute-start | bytes 98312 | tf_op jit(solution)/shard_map/ppermute | solution.py:366
  45.7 8.1 %collective-permute-start.10 = (f32[2,32,128]{2,1,0:T(8,128)S(1)}, f32[2,32,128]{2,1,0:T(8,128)S(1)}, u32[]{:S(2)}, u32[]{:S(2)}) collective-permute-start(f32[2,32,128]{2,1,0:T(8,128)S(1)} %get-tuple-element.26), channel_id=1, source_target_pairs={{0,184},{1,185},{2,186},{3,187},{4,188},{5,189},{6,190},{7,191},{8... | collective-permute-start | bytes 98312 | tf_op jit(solution)/shard_map/ppermute | solution.py:366

commit v5 on v4

--- a/solution.py
+++ b/solution.py
@@ -18,8 +18,7 @@
 STEPS = WIN // 8
 PAD = 8
 ROWS = WIN + 2 * PAD
-IMAGE = 4
-COMPS = 2
+IMAGE = 8
 LIMIT = 32
 LANES = 128
 HALVES = NY // LANES
@@ -160,13 +159,13 @@
                 field[k, comp, half, pl.ds(at, 8), :] = w
 
 
-def stencils(field, tiles=STEPS, top=0):
+def stencils(field, tiles=STEPS, top=0, together=4):
     def some(step, carry):
-        for part in range(COMPS):
-            stencil(field, COMPS * step + part, tiles, top)
+        for part in range(together):
+            stencil(field, together * step + part, tiles, top)
         return carry
 
-    lax.fori_loop(0, 4 // COMPS, some, 0)
+    lax.fori_loop(0, 4 // together, some, 0)
 
 
 def clear_ends(field):
@@ -187,7 +186,7 @@
                 lo, hi = fields[n, part, r : r + 8, 0:LANES], fields[n, part, r : r + 8, LANES:NY]
                 for half, v in enumerate(by_parity(lo, hi)):
                     field[0, 2 * n + part, half, PAD + r : PAD + r + 8, :] = v
-    stencils(field)
+    stencils(field, together=2)
 
 
 def all_levels(place, first, w0, w1, w2, w3, coef, keep, send, field, cls, table):
@@ -206,8 +205,8 @@
     def finish(level, terms, tiles, top):
         def combine(step, carry):
             places = []
-            for part in range(tiles // 2):
-                r = pl.multiple_of(PAD + top + 8 * (tiles // 2 * step + part), 8)
+            for part in range(tiles):
+                r = pl.multiple_of(PAD + top + 8 * (tiles * step + part), 8)
                 places += [(half, r) for half in range(HALVES)]
 
             def look_up(half, r):
@@ -234,7 +233,7 @@
                 field[0, 3, half, pl.ds(r, 8), :] = p[3] + s[2]
             return carry
 
-        lax.fori_loop(0, 2, combine, 0)
+        combine(0, 0)
         lb = level >> 1
         e = (level ^ lb) & 1
 

time: 54.7 us -> 55.8 us (1.020)
  Pallas kernels: 11.9 us -> 13 us
    pallas_call x1, Pallas kernels: 7.23 us -> 8.37 us  [per_device(): call(all_levels, [half_image, half_image], [SCALARS] + [LOCAL] * 6, [pltp...]
where the time goes in v5:
time: 55.8 us; the launch traced here: 55.7 us
  starting transfers between devices  22 us (39%)
  waiting for transfers between devices  19.1 us (34%)
  Pallas kernels  13 us (23%)
  between operations  0.76 us (1%)
    ppermute x6, starting transfers between devices, per_device(): lax.ppermute(mine[t * part:(t + 1) * part], AXES, axis(t))  10.4 us
    ppermute x6, waiting for transfers between devices, per_device(): lax.ppermute(mine[t * part:(t + 1) * part], AXES, axis(t))  10.1 us
    pallas_call x1, Pallas kernels, per_device(): call(all_levels, [half_image, half_image], [SCALARS] + [LOCAL] * 6, [pltp...  8.37 us
    ppermute x2, starting transfers between devices, per_device(): got = [lax.ppermute(sent[p], AXES, to_owner(p)) for p in (0, 1)]  4.96 us
    ppermute x2, waiting for transfers between devices, per_device(): got = [lax.ppermute(sent[p], AXES, to_owner(p)) for p in (0, 1)]  4.5 us
    ppermute x1, starting transfers between devices, per_device(): lax.ppermute(two, AXES, along_z(lambda c: 2 if c == 0 else -2))  3.35 us
    ppermute x1, starting transfers between devices, per_device(): lax.ppermute(up, AXES, along_z(lambda c: 1))  3.13 us
    ppermute x1, waiting for transfers between devices, per_device(): mine = keep + lax.ppermute(send, AXES, CORE_SWAP)  2.65 us
  transfers between devices with their start and end apart: 12, of which 12 were waited for; matrix products, arithmetic and copies ran while one was open for 1% of the time, Pallas kernels for 3%

profile of v5, /device:TPU:32, one launch (start us, length us, event | category | flops | bytes accessed | tf_op | source)
XLA Modules:
  0.0 55.7 jit_solution(18217886298837531779)
XLA Ops:
  0.0 0.0 copy-start
  0.0 0.1 stack.51.place
  0.1 2.0 %shard_map.55 = (s32[2,112,128]{2,1,0:T(8,128)S(1)}, s32[2,112,128]{2,1,0:T(8,128)S(1)}, s32[2,112,128]{2,1,0:T(8,128)S(1)}, s32[2,112,128]{2,1,0:T(8,128)S(1)}, f32[2,2,112,256]{3,2,1,0:T(8,128)S(1)}) custom-call(s32[12]{0:T(128)S(1)} %stack.51.place, s32[1,256,256]{2,1,0:T(8,128)} %classes.1, f32[1,2,256,256]{3,2,1,0:T(8,128)} %src.1, f32[1,2,256,256]{3,2,1,0:T(8,128)} %rec.1), custom_call_target="tpu_custom_call" | custom-call | tf_op jit(solution)/shard_map/pallas_call | solution.py:318
  2.1 3.3 %collective-permute-start = (s32[2,112,128]{2,1,0:T(8,128)S(1)}, s32[2,112,128]{2,1,0:T(8,128)S(1)}, u32[]{:S(2)}, u32[]{:S(2)}) collective-permute-start(s32[2,112,128]{2,1,0:T(8,128)S(1)} %get-tuple-element.14), channel_id=1, source_target_pairs={{0,128},{1,161},{2,130},{3,163},{4,132},{5,165},{6,134},{7,167},{8... | collective-permute-start | bytes 344072 | tf_op jit(solution)/shard_map/ppermute | solution.py:331
  5.5 3.1 %collective-permute-start.1 = (s32[2,112,128]{2,1,0:T(8,128)S(1)}, s32[2,112,128]{2,1,0:T(8,128)S(1)}, u32[]{:S(2)}, u32[]{:S(2)}) collective-permute-start(s32[2,112,128]{2,1,0:T(8,128)S(1)} %get-tuple-element.15), channel_id=1, source_target_pairs={{0,64},{1,65},{2,66},{3,67},{4,68},{5,69},{6,70},{7,71},{8,72},{9,... | collective-permute-start | bytes 344072 | tf_op jit(solution)/shard_map/ppermute | solution.py:332
  8.6 0.0 collective-permute-start.2
  9.3 0.0 copy-done
  9.3 0.2 constant_dynamic-slice_fusion
  9.4 0.1 copy.6
  9.6 1.9 %shard_map.56.first = f32[6,4,2,128,128]{4,3,2,1,0:T(8,128)S(1)} custom-call(f32[2,2,112,256]{3,2,1,0:T(8,128)S(1)} %get-tuple-element.12.fields), custom_call_target="tpu_custom_call" | custom-call | flops 10000000 | bytes 4194304 | tf_op jit(solution)/shard_map/pallas_call | solution.py:338
  11.5 0.3 collective-permute-done.w1
  11.8 0.7 %collective-permute-done.1.w2 = s32[2,112,128]{2,1,0:T(8,128)S(1)} collective-permute-done((s32[2,112,128]{2,1,0:T(8,128)S(1)}, s32[2,112,128]{2,1,0:T(8,128)S(1)}, u32[]{:S(2)}, u32[]{:S(2)}) %collective-permute-start.1) | collective-permute-done | bytes 114720 | tf_op jit(solution)/shard_map/ppermute | solution.py:332
  12.5 0.9 %collective-permute-done.2.w3 = s32[2,112,128]{2,1,0:T(8,128)S(1)} collective-permute-done((s32[2,112,128]{2,1,0:T(8,128)S(1)}, s32[2,112,128]{2,1,0:T(8,128)S(1)}, u32[]{:S(2)}, u32[]{:S(2)}) %collective-permute-start.2) | collective-permute-done | bytes 114720 | tf_op jit(solution)/shard_map/ppermute | solution.py:333
  13.4 8.4 %shard_map.57 = (f32[32,2,32,128]{3,2,1,0:T(8,128)S(1)}, f32[32,2,32,128]{3,2,1,0:T(8,128)S(1)}) custom-call(s32[12]{0:T(128)S(1)} %stack.51.place, f32[6,4,2,128,128]{4,3,2,1,0:T(8,128)S(1)} %shard_map.56.first, s32[2,112,128]{2,1,0:T(8,128)S(1)} %get-tuple-element.13.w0, s32[2,112,128]{2,1,0:T(8,128)S(1)} %collective-permute-done.w1, ...), custom_call_target="tpu_custom_call" | custom-call | flops 50000000 | bytes 4194304 | tf_op jit(solution)/shard_map/pallas_call | solution.py:346
  21.8 0.1 collective-permute-start.3
  21.9 2.6 %collective-permute-done.3 = f32[32,2,32,128]{3,2,1,0:T(8,128)S(1)} collective-permute-done((f32[32,2,32,128]{3,2,1,0:T(8,128)S(1)}, f32[32,2,32,128]{3,2,1,0:T(8,128)S(1)}, u32[]{:S(2)}, u32[]{:S(2)}) %collective-permute-start.3) | collective-permute-done | bytes 1048608 | tf_op jit(solution)/shard_map/ppermute | solution.py:359
  24.5 0.2 add.106
  24.7 0.1 fusion.4
  24.8 1.6 %collective-permute-start.4 = (f32[8,2,32,128]{3,2,1,0:T(8,128)S(1)}, f32[8,2,32,128]{3,2,1,0:T(8,128)S(1)}, u32[]{:S(2)}, u32[]{:S(2)}) collective-permute-start(f32[8,2,32,128]{3,2,1,0:T(8,128)S(1)} %get-tuple-element.19), channel_id=1, source_target_pairs={{0,8},{1,3},{2,10},{3,5},{4,12},{5,7},{6,14},{7,1},{8,16},{9,11},{... | collective-permute-start | bytes 786440 | tf_op jit(solution)/shard_map/ppermute | solution.py:362
  26.4 1.7 %collective-permute-start.6 = (f32[8,2,32,128]{3,2,1,0:T(8,128)S(1)}, f32[8,2,32,128]{3,2,1,0:T(8,128)S(1)}, u32[]{:S(2)}, u32[]{:S(2)}) collective-permute-start(f32[8,2,32,128]{3,2,1,0:T(8,128)S(1)} %get-tuple-element.20), channel_id=1, source_target_pairs={{0,24},{1,7},{2,26},{3,1},{4,28},{5,3},{6,30},{7,5},{8,0},{9,15},{... | collective-permute-start | bytes 786440 | tf_op jit(solution)/shard_map/ppermute | solution.py:362
  28.1 1.8 %collective-permute-start.5 = (f32[8,2,32,128]{3,2,1,0:T(8,128)S(1)}, f32[8,2,32,128]{3,2,1,0:T(8,128)S(1)}, u32[]{:S(2)}, u32[]{:S(2)}) collective-permute-start(f32[8,2,32,128]{3,2,1,0:T(8,128)S(1)} %get-tuple-element.21), channel_id=1, source_target_pairs={{0,16},{1,5},{2,18},{3,7},{4,20},{5,1},{6,22},{7,3},{8,24},{9,13},... | collective-permute-start | bytes 786440 | tf_op jit(solution)/shard_map/ppermute | solution.py:362
  29.9 2.5 %collective-permute-done.4 = f32[8,2,32,128]{3,2,1,0:T(8,128)S(1)} collective-permute-done((f32[8,2,32,128]{3,2,1,0:T(8,128)S(1)}, f32[8,2,32,128]{3,2,1,0:T(8,128)S(1)}, u32[]{:S(2)}, u32[]{:S(2)}) %collective-permute-start.4) | collective-permute-done | bytes 262176 | tf_op jit(solution)/shard_map/ppermute | solution.py:362
  32.5 2.4 %collective-permute-done.6 = f32[8,2,32,128]{3,2,1,0:T(8,128)S(1)} collective-permute-done((f32[8,2,32,128]{3,2,1,0:T(8,128)S(1)}, f32[8,2,32,128]{3,2,1,0:T(8,128)S(1)}, u32[]{:S(2)}, u32[]{:S(2)}) %collective-permute-start.6) | collective-permute-done | bytes 262176 | tf_op jit(solution)/shard_map/ppermute | solution.py:362
  34.9 1.4 %collective-permute-done.5 = f32[8,2,32,128]{3,2,1,0:T(8,128)S(1)} collective-permute-done((f32[8,2,32,128]{3,2,1,0:T(8,128)S(1)}, f32[8,2,32,128]{3,2,1,0:T(8,128)S(1)}, u32[]{:S(2)}, u32[]{:S(2)}) %collective-permute-start.5) | collective-permute-done | bytes 262176 | tf_op jit(solution)/shard_map/ppermute | solution.py:362
  36.3 0.1 fusion.1
  36.4 1.7 %collective-permute-start.7 = (f32[2,2,32,128]{3,2,1,0:T(8,128)S(1)}, f32[2,2,32,128]{3,2,1,0:T(8,128)S(1)}, u32[]{:S(2)}, u32[]{:S(2)}) collective-permute-start(f32[2,2,32,128]{3,2,1,0:T(8,128)S(1)} %get-tuple-element.22), channel_id=1, source_target_pairs={{0,2},{1,9},{2,4},{3,11},{4,6},{5,13},{6,0},{7,15},{8,10},{9,17},{... | collective-permute-start | bytes 196616 | tf_op jit(solution)/shard_map/ppermute | solution.py:362
  38.0 1.7 %collective-permute-start.9 = (f32[2,2,32,128]{3,2,1,0:T(8,128)S(1)}, f32[2,2,32,128]{3,2,1,0:T(8,128)S(1)}, u32[]{:S(2)}, u32[]{:S(2)}) collective-permute-start(f32[2,2,32,128]{3,2,1,0:T(8,128)S(1)} %get-tuple-element.23), channel_id=1, source_target_pairs={{0,6},{1,25},{2,0},{3,27},{4,2},{5,29},{6,4},{7,31},{8,14},{9,1},{... | collective-permute-start | bytes 196616 | tf_op jit(solution)/shard_map/ppermute | solution.py:362
  39.7 2.0 %collective-permute-start.8 = (f32[2,2,32,128]{3,2,1,0:T(8,128)S(1)}, f32[2,2,32,128]{3,2,1,0:T(8,128)S(1)}, u32[]{:S(2)}, u32[]{:S(2)}) collective-permute-start(f32[2,2,32,128]{3,2,1,0:T(8,128)S(1)} %get-tuple-element.24), channel_id=1, source_target_pairs={{0,4},{1,17},{2,6},{3,19},{4,0},{5,21},{6,2},{7,23},{8,12},{9,25},... | collective-permute-start | bytes 196616 | tf_op jit(solution)/shard_map/ppermute | solution.py:362
  41.7 0.3 collective-permute-done.7
  41.9 0.4 collective-permute-done.9
  42.3 3.2 %collective-permute-done.8 = f32[2,2,32,128]{3,2,1,0:T(8,128)S(1)} collective-permute-done((f32[2,2,32,128]{3,2,1,0:T(8,128)S(1)}, f32[2,2,32,128]{3,2,1,0:T(8,128)S(1)}, u32[]{:S(2)}, u32[]{:S(2)}) %collective-permute-start.8) | collective-permute-done | bytes 65568 | tf_op jit(solution)/shard_map/ppermute | solution.py:362
  45.5 1.3 %collective-permute-start.11 = (f32[2,32,128]{2,1,0:T(8,128)S(1)}, f32[2,32,128]{2,1,0:T(8,128)S(1)}, u32[]{:S(2)}, u32[]{:S(2)}) collective-permute-start(f32[2,32,128]{2,1,0:T(8,128)S(1)} %get-tuple-element.25), channel_id=1, source_target_pairs={{0,120},{1,121},{2,122},{3,123},{4,124},{5,125},{6,126},{7,127},{8... | collective-permute-start | bytes 98312 | tf_op jit(solution)/shard_map/ppermute | solution.py:365
  46.8 3.6 %collective-permute-start.10 = (f32[2,32,128]{2,1,0:T(8,128)S(1)}, f32[2,32,128]{2,1,0:T(8,128)S(1)}, u32[]{:S(2)}, u32[]{:S(2)}) collective-permute-start(f32[2,32,128]{2,1,0:T(8,128)S(1)} %get-tuple-element.26), channel_id=1, source_target_pairs={{0,184},{1,185},{2,186},{3,187},{4,188},{5,189},{6,190},{7,191},{8... | collective-permute-start | bytes 98312 | tf_op jit(solution)/shard_map/ppermute | solution.py:365
  50.5 0.2 collective-permute-done.11.b
  50.7 4.3 %collective-permute-done.10.a = f32[2,32,128]{2,1,0:T(8,128)S(1)} collective-permute-done((f32[2,32,128]{2,1,0:T(8,128)S(1)}, f32[2,32,128]{2,1,0:T(8,128)S(1)}, u32[]{:S(2)}, u32[]{:S(2)}) %collective-permute-start.10) | collective-permute-done | bytes 32800 | tf_op jit(solution)/shard_map/ppermute | solution.py:365
  55.0 0.7 %shard_map.58 = f32[4,1,8,256]{3,2,1,0:T(8,128)} custom-call(f32[2,32,128]{2,1,0:T(8,128)S(1)} %collective-permute-done.10.a, f32[2,32,128]{2,1,0:T(8,128)S(1)} %collective-permute-done.11.b), custom_call_target="tpu_custom_call" | custom-call | tf_op jit(solution)/shard_map/pallas_call | solution.py:366
  (6 shorter events, 0.1 us)
Async XLA Ops:
  0.0 9.3 %copy-start = (f32[16,64,2,6]{1,2,3,0:T(2,128)S(1)}, f32[16,64,2,6]{1,2,3,0:T(2,128)}, u32[]{:S(2)}) copy-start(f32[16,64,2,6]{1,2,3,0:T(2,128)} %param.8) | copy-start | bytes 147460
  2.1 9.7 %collective-permute-start = (s32[2,112,128]{2,1,0:T(8,128)S(1)}, s32[2,112,128]{2,1,0:T(8,128)S(1)}, u32[]{:S(2)}, u32[]{:S(2)}) collective-permute-start(s32[2,112,128]{2,1,0:T(8,128)S(1)} %get-tuple-element.14), channel_id=1, source_target_pairs={{0,128},{1,161},{2,130},{3,163},{4,132},{5,165},{6,134},{7,167},{8... | collective-permute-start | bytes 344072 | tf_op jit(solution)/shard_map/ppermute | solution.py:331
  5.5 7.0 %collective-permute-start.1 = (s32[2,112,128]{2,1,0:T(8,128)S(1)}, s32[2,112,128]{2,1,0:T(8,128)S(1)}, u32[]{:S(2)}, u32[]{:S(2)}) collective-permute-start(s32[2,112,128]{2,1,0:T(8,128)S(1)} %get-tuple-element.15), channel_id=1, source_target_pairs={{0,64},{1,65},{2,66},{3,67},{4,68},{5,69},{6,70},{7,71},{8,72},{9,... | collective-permute-start | bytes 344072 | tf_op jit(solution)/shard_map/ppermute | solution.py:332
  8.6 4.8 %collective-permute-start.2 = (s32[2,112,128]{2,1,0:T(8,128)S(1)}, s32[2,112,128]{2,1,0:T(8,128)S(1)}, u32[]{:S(2)}, u32[]{:S(2)}) collective-permute-start(s32[2,112,128]{2,1,0:T(8,128)S(1)} %get-tuple-element.16), channel_id=1, source_target_pairs={{0,224},{1,225},{2,226},{3,227},{4,228},{5,229},{6,230},{7,231},{8... | collective-permute-start | bytes 344072 | tf_op jit(solution)/shard_map/ppermute | solution.py:333
  21.8 2.7 %collective-permute-start.3 = (f32[32,2,32,128]{3,2,1,0:T(8,128)S(1)}, f32[32,2,32,128]{3,2,1,0:T(8,128)S(1)}, u32[]{:S(2)}, u32[]{:S(2)}) collective-permute-start(f32[32,2,32,128]{3,2,1,0:T(8,128)S(1)} %get-tuple-element.18), channel_id=1, source_target_pairs={{0,1},{1,0},{2,3},{3,2},{4,5},{5,4},{6,7},{7,6},{8,9},{9,8},{10,11... | collective-permute-start | bytes 3145736 | tf_op jit(solution)/shard_map/ppermute | solution.py:359
  24.8 7.7 %collective-permute-start.4 = (f32[8,2,32,128]{3,2,1,0:T(8,128)S(1)}, f32[8,2,32,128]{3,2,1,0:T(8,128)S(1)}, u32[]{:S(2)}, u32[]{:S(2)}) collective-permute-start(f32[8,2,32,128]{3,2,1,0:T(8,128)S(1)} %get-tuple-element.19), channel_id=1, source_target_pairs={{0,8},{1,3},{2,10},{3,5},{4,12},{5,7},{6,14},{7,1},{8,16},{9,11},{... | collective-permute-start | bytes 786440 | tf_op jit(solution)/shard_map/ppermute | solution.py:362
  26.4 8.5 %collective-permute-start.6 = (f32[8,2,32,128]{3,2,1,0:T(8,128)S(1)}, f32[8,2,32,128]{3,2,1,0:T(8,128)S(1)}, u32[]{:S(2)}, u32[]{:S(2)}) collective-permute-start(f32[8,2,32,128]{3,2,1,0:T(8,128)S(1)} %get-tuple-element.20), channel_id=1, source_target_pairs={{0,24},{1,7},{2,26},{3,1},{4,28},{5,3},{6,30},{7,5},{8,0},{9,15},{... | collective-permute-start | bytes 786440 | tf_op jit(solution)/shard_map/ppermute | solution.py:362
  28.1 8.1 %collective-permute-start.5 = (f32[8,2,32,128]{3,2,1,0:T(8,128)S(1)}, f32[8,2,32,128]{3,2,1,0:T(8,128)S(1)}, u32[]{:S(2)}, u32[]{:S(2)}) collective-permute-start(f32[8,2,32,128]{3,2,1,0:T(8,128)S(1)} %get-tuple-element.21), channel_id=1, source_target_pairs={{0,16},{1,5},{2,18},{3,7},{4,20},{5,1},{6,22},{7,3},{8,24},{9,13},... | collective-permute-start | bytes 786440 | tf_op jit(solution)/shard_map/ppermute | solution.py:362
  36.4 5.6 %collective-permute-start.7 = (f32[2,2,32,128]{3,2,1,0:T(8,128)S(1)}, f32[2,2,32,128]{3,2,1,0:T(8,128)S(1)}, u32[]{:S(2)}, u32[]{:S(2)}) collective-permute-start(f32[2,2,32,128]{3,2,1,0:T(8,128)S(1)} %get-tuple-element.22), channel_id=1, source_target_pairs={{0,2},{1,9},{2,4},{3,11},{4,6},{5,13},{6,0},{7,15},{8,10},{9,17},{... | collective-permute-start | bytes 196616 | tf_op jit(solution)/shard_map/ppermute | solution.py:362
  38.0 4.3 %collective-permute-start.9 = (f32[2,2,32,128]{3,2,1,0:T(8,128)S(1)}, f32[2,2,32,128]{3,2,1,0:T(8,128)S(1)}, u32[]{:S(2)}, u32[]{:S(2)}) collective-permute-start(f32[2,2,32,128]{3,2,1,0:T(8,128)S(1)} %get-tuple-element.23), channel_id=1, source_target_pairs={{0,6},{1,25},{2,0},{3,27},{4,2},{5,29},{6,4},{7,31},{8,14},{9,1},{... | collective-permute-start | bytes 196616 | tf_op jit(solution)/shard_map/ppermute | solution.py:362
  39.7 5.8 %collective-permute-start.8 = (f32[2,2,32,128]{3,2,1,0:T(8,128)S(1)}, f32[2,2,32,128]{3,2,1,0:T(8,128)S(1)}, u32[]{:S(2)}, u32[]{:S(2)}) collective-permute-start(f32[2,2,32,128]{3,2,1,0:T(8,128)S(1)} %get-tuple-element.24), channel_id=1, source_target_pairs={{0,4},{1,17},{2,6},{3,19},{4,0},{5,21},{6,2},{7,23},{8,12},{9,25},... | collective-permute-start | bytes 196616 | tf_op jit(solution)/shard_map/ppermute | solution.py:362
  45.5 5.2 %collective-permute-start.11 = (f32[2,32,128]{2,1,0:T(8,128)S(1)}, f32[2,32,128]{2,1,0:T(8,128)S(1)}, u32[]{:S(2)}, u32[]{:S(2)}) collective-permute-start(f32[2,32,128]{2,1,0:T(8,128)S(1)} %get-tuple-element.25), channel_id=1, source_target_pairs={{0,120},{1,121},{2,122},{3,123},{4,124},{5,125},{6,126},{7,127},{8... | collective-permute-start | bytes 98312 | tf_op jit(solution)/shard_map/ppermute | solution.py:365
  46.8 8.1 %collective-permute-start.10 = (f32[2,32,128]{2,1,0:T(8,128)S(1)}, f32[2,32,128]{2,1,0:T(8,128)S(1)}, u32[]{:S(2)}, u32[]{:S(2)}) collective-permute-start(f32[2,32,128]{2,1,0:T(8,128)S(1)} %get-tuple-element.26), channel_id=1, source_target_pairs={{0,184},{1,185},{2,186},{3,187},{4,188},{5,189},{6,190},{7,191},{8... | collective-permute-start | bytes 98312 | tf_op jit(solution)/shard_map/ppermute | solution.py:365
